TPU v7x, 1024 devices: a whole 4x8x16 slice. The times are simulated.
1024 devices in a mesh: lat: 32 (over x, y), lon: 8 (over z_hi, core), lev: 4 (over z_lo).
Axes of the slice: x: 4, y: 8, z: 16 (z_hi: 4, z_lo: 4; z = z_hi * 4 + z_lo), core: 2. Of those that a mesh axis runs over, the one named last changes fastest.
Arguments:
- adjoint_u: float32 [4, 512, 3600], P('lev', 'lat', 'lon'), may hold values from -6 to 6
- adjoint_v: float32 [4, 512, 3600], P('lev', 'lat', 'lon'), may hold values from -6 to 6
- adjoint_temp: float32 [4, 512, 3600], P('lev', 'lat', 'lon'), may hold values from -6 to 6
- adjoint_pres: float32 [512, 3600], P('lat', 'lon'), may hold values from -6 to 6
- carrying_eastward_flow: float32 [4, 512, 3600], P('lev', 'lat', 'lon'), may hold values from -4 to 4
- cutoff: int32 [2, 64], replicated, may hold values from 3 to 559, as said below
Outputs:
- prior_u: float32 [4, 512, 3600], P('lev', 'lat', 'lon')
- prior_v: float32 [4, 512, 3600], P('lev', 'lat', 'lon')
- prior_temp: float32 [4, 512, 3600], P('lev', 'lat', 'lon')
- prior_pres: float32 [512, 3600], P('lat', 'lon')
Inputs may be any that keep to these rules, and one draw needn't show every extreme that they name: cutoff[h, r] belongs to the row r rows away from the south (h = 0) or north (h = 1) pole and lies between max(1, w // 2) and w - 1, with w = 2 + (5 * 3600 * (2 r + 1)) // 4096; both ends of the overall range are reached in every draw.
All inputs are finite; a program needn't handle non-finite values.
Results may differ from a plain program's by a relative error of at most 0.0002.
Values sent between devices are 32-bit elements; how exact they have to be, the bound alone decides.
A program may use at most 32 MiB of HBM per device.

v0:
```python
import math

import jax
import jax.numpy as jnp
from jax import lax
from jax.sharding import PartitionSpec as P

zonal_courant = 0.15
merid_courant = 0.15
coriolis_scale = 0.4
heat_link_multiplier = 0.3


def with_halo(shard, sides, width, wrap):
    for axis, dim in sides:
        size, length = (lax.axis_size(axis), shard.shape[dim])
        up = [(i, (i + 1) % size) for i in range(size if wrap else size - 1)]
        down = [(j, i) for i, j in up]
        last = lax.slice_in_dim(shard, length - width, length, axis=dim)
        initial = lax.slice_in_dim(shard, 0, width, axis=dim)
        before = lax.ppermute(last, axis, up)
        after = lax.ppermute(initial, axis, down)
        shard = jnp.concatenate([before, shard, after], axis=dim)
    return shard


def shifted(value, axis, steps):
    count = lax.axis_size(axis)
    pairs = [(source, (source + steps) % count) for source in range(count)]
    return lax.ppermute(value, axis, pairs)


def split_factor(length):
    divisor = math.isqrt(length)
    while length % divisor != 0:
        divisor = divisor - 1
    return divisor


def wave_tables(length):
    wave_index = jnp.arange(length, dtype=jnp.int32)
    phase_step = wave_index[:, None] * wave_index[None, :] % length
    angles = phase_step.astype(jnp.float32) * (2.0 * math.pi / length)
    return (jnp.cos(angles), jnp.sin(angles))


def contract(pattern, left_side, right_side):
    return jnp.einsum(pattern, left_side, right_side, precision=lax.Precision.HIGHEST)


def filter_circles(circles, latitude_harmonic_limit):
    row_count, length = circles.shape
    outer_size = split_factor(length)
    inner_size = length // outer_size
    cos_outer, sin_outer = wave_tables(outer_size)
    cos_inner, sin_inner = wave_tables(inner_size)
    first_index = jnp.arange(outer_size, dtype=jnp.int32)[:, None]
    second_index = jnp.arange(inner_size, dtype=jnp.int32)[None, :]
    twist_angle = (first_index * second_index % length).astype(jnp.float32) * (
        2.0 * math.pi / length
    )
    twist_cos = jnp.cos(twist_angle)
    twist_sin = jnp.sin(twist_angle)
    blocks = circles.reshape(row_count, outer_size, inner_size)
    real_a = contract("mab,ak->mkb", blocks, cos_outer)
    imag_a = -contract("mab,ak->mkb", blocks, sin_outer)
    real_b = real_a * twist_cos + imag_a * twist_sin
    imag_b = imag_a * twist_cos - real_a * twist_sin
    real_x = contract("mkb,bj->mkj", real_b, cos_inner) + contract("mkb,bj->mkj", imag_b, sin_inner)
    imag_x = contract("mkb,bj->mkj", imag_b, cos_inner) - contract("mkb,bj->mkj", real_b, sin_inner)
    wave_number = first_index + outer_size * second_index
    wave_number = jnp.minimum(wave_number, length - wave_number).astype(jnp.float32)[None]
    cut_float = latitude_harmonic_limit.astype(jnp.float32)[:, None, None]
    factor = (
        jnp.where(wave_number <= cut_float, 1.0, (cut_float / jnp.maximum(wave_number, 1.0)) ** 2)
        / length
    )
    real_x = real_x * factor
    imag_x = imag_x * factor
    real_y = contract("mkj,bj->mkb", real_x, cos_inner) - contract("mkj,bj->mkb", imag_x, sin_inner)
    imag_y = contract("mkj,bj->mkb", imag_x, cos_inner) + contract("mkj,bj->mkb", real_x, sin_inner)
    real_z = real_y * twist_cos - imag_y * twist_sin
    imag_z = imag_y * twist_cos + real_y * twist_sin
    result = contract("mkb,ak->mab", real_z, cos_outer) - contract("mkb,ak->mab", imag_z, sin_outer)
    return result.reshape(row_count, length)


def cutoff_of_rows(cutoff, row_index, total_rows, length):
    polar_count = cutoff.shape[1]
    pole_rank = jnp.arange(polar_count, dtype=jnp.int32)
    south_cut = jnp.sum(
        cutoff[0][None, :] * (row_index[:, None] == pole_rank[None, :]).astype(jnp.int32), axis=1
    )
    north_cut = jnp.sum(
        cutoff[1][None, :]
        * (row_index[:, None] == total_rows - 1 - pole_rank[None, :]).astype(jnp.int32),
        axis=1,
    )
    polar_row = (row_index < polar_count) | (row_index >= total_rows - polar_count)
    return jnp.where(polar_row, south_cut + north_cut, length)


def local(adjoint_u, adjoint_v, adjoint_temp, adjoint_pres, carrying_eastward_flow, cutoff):
    levels, lat_rows, lon_width = adjoint_u.shape
    lat_devs = lax.axis_size("lat")
    lon_devs = lax.axis_size("lon")
    total_rows = lat_rows * lat_devs
    total_levels = levels * lax.axis_size("lev")
    circle_length = lon_width * lon_devs
    lat_position = lax.axis_index("lat")
    row_index = lat_position * lat_rows + jnp.arange(lat_rows, dtype=jnp.int32)
    latitude = ((row_index.astype(jnp.float32) + 0.5) / total_rows - 0.5) * jnp.pi
    eastward_scale_weight = (zonal_courant / jnp.cos(latitude))[:, None]
    coriolis = (coriolis_scale * jnp.sin(latitude))[:, None]
    latitude_harmonic_limit = cutoff_of_rows(cutoff, row_index, total_rows, circle_length)
    tiled_cut = jnp.tile(latitude_harmonic_limit, 3 * levels)
    stacked = jnp.stack([adjoint_u, adjoint_v, adjoint_temp]).reshape(
        3 * levels * lat_rows, lon_width
    )
    circles = lax.all_gather(stacked, "lon", axis=1, tiled=True)
    filtered = filter_circles(circles, tiled_cut)
    offset = lax.axis_index("lon") * lon_width
    local_part = lax.dynamic_slice_in_dim(filtered, offset, lon_width, 1)
    smooth = local_part.reshape(3, levels, lat_rows, lon_width)
    filtered_u = smooth[0]
    filtered_v = smooth[1]
    filtered_t = smooth[2]
    div_bar = -heat_link_multiplier * filtered_t - adjoint_pres[None] / total_levels
    advect = carrying_eastward_flow * filtered_t
    zonal_in = jnp.stack([div_bar, filtered_u, advect])
    zonal_pad = with_halo(zonal_in, (("lon", 3),), 1, True)
    zonal_diff = zonal_pad[..., 2:] - zonal_pad[..., :-2]
    merid_in = jnp.stack([div_bar, filtered_v])
    merid_pad = with_halo(merid_in, (("lat", 2),), 1, False)
    edge_rows = jnp.stack([merid_in[:, :, 0, :], merid_in[:, :, -1, :]], axis=2)
    across = shifted(edge_rows, "lon", lon_devs // 2)
    ghost_sign = jnp.array([1.0, -1.0], jnp.float32)[:, None, None, None]
    south_ghost = jnp.where(
        lat_position == 0, ghost_sign * across[:, :, 0:1, :], merid_pad[:, :, :1, :]
    )
    north_ghost = jnp.where(
        lat_position == lat_devs - 1, ghost_sign * across[:, :, 1:2, :], merid_pad[:, :, -1:, :]
    )
    extended = jnp.concatenate([south_ghost, merid_pad[:, :, 1:-1, :], north_ghost], axis=2)
    merid_diff = extended[:, :, 2:, :] - extended[:, :, :-2, :]
    height_bar = eastward_scale_weight * zonal_diff[1] + merid_courant * merid_diff[1]
    prior_u = adjoint_u - coriolis * filtered_v - eastward_scale_weight * zonal_diff[0]
    prior_v = adjoint_v + coriolis * filtered_u - merid_courant * merid_diff[0]
    prior_temp = adjoint_temp + height_bar + eastward_scale_weight * zonal_diff[2]
    column_sum = lax.psum(jnp.sum(height_bar, axis=0), "lev")
    prior_pres = adjoint_pres + column_sum
    return (prior_u, prior_v, prior_temp, prior_pres)


def solution(mesh):
    in_specs = (
        P("lev", "lat", "lon"),
        P("lev", "lat", "lon"),
        P("lev", "lat", "lon"),
        P("lat", "lon"),
        P("lev", "lat", "lon"),
        P(),
    )
    out_specs = (
        P("lev", "lat", "lon"),
        P("lev", "lat", "lon"),
        P("lev", "lat", "lon"),
        P("lat", "lon"),
    )
    return jax.shard_map(local, mesh=mesh, in_specs=in_specs, out_specs=out_specs, check_vma=False)
```

profile of v0, /device:TPU:58, one launch (start us, length us, event | category | flops | bytes accessed | tf_op | source)
XLA Modules:
  0.0 117.0 jit_solution(1660836250095537827)
XLA Ops:
  0.8 0.8 pad_maximum_fusion.6
  1.6 34.9 %all-gather = f32[8,450,48]{1,2,0:T(8,128)S(1)} all-gather(f32[1,450,48]{1,2,0:T(8,128)S(1)} %bitcast.118), channel_id=1, replica_groups=mesh['lat'=32,'lon'=8,'lev'=4] {'lon'}, dimensions={0}, use_global_device_ids=true | all-gather | bytes 777600 | tf_op jit(solution)/shard_map/all_gather | solution.py:120
  37.4 2.2 %reshape.292 = f32[48,60,60]{2,1,0:T(8,128)S(1)} reshape(f32[48,3600]{1,0:T(8,128)S(1)} %bitcast.117) | data formatting | bytes 1382400 | tf_op jit(solution)/shard_map/reshape | solution.py:64
  39.6 1.6 %convolution_negate_fusion = f32[60,48,60]{2,0,1:T(8,128)S(1)} fusion(f32[48,60,60]{2,1,0:T(8,128)S(1)} %reshape.292), kind=kOutput, calls=%fused_computation.26 | convolution fusion | flops 124621200 | bytes 1382400 | tf_op jit(solution)/shard_map/mab,ak->mkb/dot_general | solution.py:48
  41.3 1.6 %fusion.49 = f32[60,48,60]{2,0,1:T(8,128)S(1)} fusion(f32[48,60,60]{2,1,0:T(8,128)S(1)} %reshape.292), kind=kOutput, calls=%fused_computation.77 | convolution fusion | flops 124448400 | bytes 1382400 | tf_op jit(solution)/shard_map/mab,ak->mkb/dot_general | solution.py:48
  43.0 2.7 %fusion.2 = f32[48,60,60]{2,1,0:T(8,128)} fusion(f32[60,48,60]{2,0,1:T(8,128)S(1)} %fusion.49, f32[60,48,60]{2,0,1:T(8,128)S(1)} %convolution_negate_fusion, f32[60,60]{1,0:T(8,128)S(1)} %get-tuple-element.20, f32[60,60]{1,0:T(8,128)S(1)} %get-tuple-element.21), kind=kOutput, calls=%fused_computation.3 | convolution fusion | flops 124966800 | bytes 2102400 | tf_op jit(solution)/shard_map/mkb,bj->mkj/dot_general | solution.py:48
  45.7 1.6 %fusion.4 = f32[48,60,60]{2,1,0:T(8,128)S(1)} fusion(f32[60,48,60]{2,0,1:T(8,128)S(1)} %fusion.49, f32[60,48,60]{2,0,1:T(8,128)S(1)} %convolution_negate_fusion, f32[60,60]{1,0:T(8,128)S(1)} %get-tuple-element.20, f32[60,60]{1,0:T(8,128)S(1)} %get-tuple-element.21), kind=kOutput, calls=%fused_computation.5 | convolution fusion | flops 124966800 | bytes 2102400 | tf_op jit(solution)/shard_map/mkb,bj->mkj/dot_general | solution.py:48
  47.6 3.7 %subtract_multiply_fusion = f32[48,60,60]{2,1,0:T(8,128)S(1)} fusion(f32[48,60,60]{2,1,0:T(8,128)} %fusion.2, f32[60,60]{1,0:T(8,128)S(1)} %broadcast_maximum_fusion, f32[60,60]{1,0:T(8,128)S(1)} %fusion.34, f32[48]{0:T(128)S(1)} %convert_element_type.90, f32[60,48,60]{2,0,1:T(8,128)S(1)} %convolution_negate_fusion, f32[60,48,60]{2,0,1:T(8,128)} %copy-done, ...), kind=kOutput, calls=%fused_computation.20 | convolution fusion | flops 126176400 | bytes 2822592 | tf_op jit(solution)/shard_map/mkb,bj->mkj/dot_general | solution.py:48
  51.3 1.7 %fusion.52 = f32[48,60,60]{2,1,0:T(8,128)S(1)} fusion(f32[48,60,60]{2,1,0:T(8,128)S(1)} %subtract_multiply_fusion), kind=kOutput, calls=%fused_computation.80 | convolution fusion | flops 124448400 | bytes 1382400 | tf_op jit(solution)/shard_map/mkj,bj->mkb/dot_general | solution.py:48
  53.0 1.8 %add_multiply_fusion = f32[48,60,60]{2,1,0:T(8,128)S(1)} fusion(f32[48,60,60]{2,1,0:T(8,128)S(1)} %fusion.4, f32[60,60]{1,0:T(8,128)S(1)} %broadcast_maximum_fusion, f32[60,60]{1,0:T(8,128)S(1)} %fusion.34, f32[48]{0:T(128)S(1)} %convert_element_type.90, f32[60,48,60]{2,0,1:T(8,128)S(1)} %convolution_negate_fusion, f32[60,48,60]{2,0,1:T(8,128)S(1)} %copy-done.1, ...), kind=kOutput, calls=%fused_computation.21 | convolution fusion | flops 126176400 | bytes 2822592 | tf_op jit(solution)/shard_map/mkb,bj->mkj/dot_general | solution.py:48
  54.9 1.5 %fusion.55 = f32[48,60,60]{2,1,0:T(8,128)S(1)} fusion(f32[48,60,60]{2,1,0:T(8,128)S(1)} %add_multiply_fusion), kind=kOutput, calls=%fused_computation.83 | convolution fusion | flops 124448400 | bytes 1382400 | tf_op jit(solution)/shard_map/mkj,bj->mkb/dot_general | solution.py:48
  56.4 1.6 %convolution_add_fusion = f32[48,60,60]{2,1,0:T(8,128)S(1)} fusion(f32[48,60,60]{2,1,0:T(8,128)S(1)} %fusion.52, f32[48,60,60]{2,1,0:T(8,128)S(1)} %add_multiply_fusion), kind=kOutput, calls=%fused_computation.24 | convolution fusion | flops 124621200 | bytes 2073600 | tf_op jit(solution)/shard_map/mkj,bj->mkb/dot_general | solution.py:48
  58.0 1.6 %convolution_subtract_fusion = f32[48,60,60]{2,1,0:T(8,128)S(1)} fusion(f32[48,60,60]{2,1,0:T(8,128)S(1)} %fusion.55, f32[48,60,60]{2,1,0:T(8,128)S(1)} %subtract_multiply_fusion), kind=kOutput, calls=%fused_computation.25 | convolution fusion | flops 124621200 | bytes 2073600 | tf_op jit(solution)/shard_map/mkj,bj->mkb/dot_general | solution.py:48
  59.6 1.6 %fusion.10 = f32[60,48,60]{2,0,1:T(8,128)S(1)} fusion(f32[48,60,60]{2,1,0:T(8,128)S(1)} %convolution_subtract_fusion, f32[48,60,60]{2,1,0:T(8,128)S(1)} %convolution_add_fusion, f32[60,60]{1,0:T(8,128)S(1)} %get-tuple-element.20, f32[60,60]{1,0:T(8,128)S(1)} %get-tuple-element.21), kind=kOutput, calls=%fused_computation.12 | convolution fusion | flops 124966800 | bytes 2102400 | tf_op jit(solution)/shard_map/mkb,ak->mab/dot_general | solution.py:48
  61.3 1.6 %subtract_bitcast_fusion = f32[48,60,60]{2,1,0:T(8,128)S(1)} fusion(f32[60,48,60]{2,0,1:T(8,128)S(1)} %fusion.10, f32[48,60,60]{2,1,0:T(8,128)S(1)} %convolution_add_fusion, f32[48,60,60]{2,1,0:T(8,128)S(1)} %convolution_subtract_fusion, f32[60,60]{1,0:T(8,128)S(1)} %get-tuple-element.20, f32[60,60]{1,0:T(8,128)S(1)} %get-tuple-element.21), kind=kOutput, calls=%fused_computation.11 | convolution fusion | flops 125139600 | bytes 2793600 | tf_op jit(solution)/shard_map/mkb,ak->mab/dot_general | solution.py:48
  63.0 1.0 reshape.293
  64.3 6.1 %collective-permute-start = (f32[3,1,16,1]{3,2,1,0:T(8,128)S(1)}, f32[3,1,16,1]{3,2,1,0:T(8,128)S(1)}, u32[]{:S(2)}, u32[]{:S(2)}) collective-permute-start(f32[3,1,16,1]{3,2,1,0:T(8,128)S(1)} %get-tuple-element.12), channel_id=1, source_target_pairs={{4,0},{8,4},{12,8},{16,12},{20,16},{24,20},{28,24},{0,28},{5,1},{9... | collective-permute-start | bytes 584 | tf_op jit(solution)/shard_map/ppermute | solution.py:22
  70.3 1.9 %collective-permute-start.1 = (f32[3,1,16,1]{3,2,1,0:T(8,128)S(1)}, f32[3,1,16,1]{3,2,1,0:T(8,128)S(1)}, u32[]{:S(2)}, u32[]{:S(2)}) collective-permute-start(f32[3,1,16,1]{3,2,1,0:T(8,128)S(1)} %get-tuple-element.13), channel_id=1, source_target_pairs={{0,4},{4,8},{8,12},{12,16},{16,20},{20,24},{24,28},{28,0},{1,5},{5... | collective-permute-start | bytes 584 | tf_op jit(solution)/shard_map/ppermute | solution.py:21
  72.3 3.3 %collective-permute-start.3 = (f32[2,1,1,450]{3,2,1,0:T(1,128)S(1)}, f32[2,1,1,450]{3,2,1,0:T(1,128)S(1)}, u32[]{:S(2)}, u32[]{:S(2)}) collective-permute-start(f32[2,1,1,450]{3,2,1,0:T(1,128)S(1)} %get-tuple-element.14), channel_id=1, source_target_pairs={{32,0},{64,32},{96,64},{128,96},{160,128},{192,160},{224,192},{256... | collective-permute-start | bytes 10808 | tf_op jit(solution)/shard_map/ppermute | solution.py:22
  75.6 4.7 %collective-permute-start.4 = (f32[2,1,1,450]{3,2,1,0:T(1,128)S(1)}, f32[2,1,1,450]{3,2,1,0:T(1,128)S(1)}, u32[]{:S(2)}, u32[]{:S(2)}) collective-permute-start(f32[2,1,1,450]{3,2,1,0:T(1,128)S(1)} %get-tuple-element.15), channel_id=1, source_target_pairs={{0,32},{32,64},{64,96},{96,128},{128,160},{160,192},{192,224},{224... | collective-permute-start | bytes 10808 | tf_op jit(solution)/shard_map/ppermute | solution.py:21
  80.3 7.2 %collective-permute-start.2 = (f32[2,1,2,450]{3,2,1,0:T(2,128)S(1)}, f32[2,1,2,450]{3,2,1,0:T(2,128)S(1)}, u32[]{:S(2)}, u32[]{:S(2)}) collective-permute-start(f32[2,1,2,450]{3,2,1,0:T(2,128)S(1)} %pad_maximum_fusion.14), channel_id=1, source_target_pairs={{0,16},{4,20},{8,24},{12,28},{16,0},{20,4},{24,8},{28,12},{1,17},{... | collective-permute-start | bytes 21608 | tf_op jit(solution)/shard_map/ppermute | solution.py:30
  87.8 6.7 %collective-permute-done.2 = f32[2,1,2,450]{3,2,1,0:T(2,128)S(1)} collective-permute-done((f32[2,1,2,450]{3,2,1,0:T(2,128)S(1)}, f32[2,1,2,450]{3,2,1,0:T(2,128)S(1)}, u32[]{:S(2)}, u32[]{:S(2)}) %collective-permute-start.2) | collective-permute-done | bytes 7232 | tf_op jit(solution)/shard_map/ppermute | solution.py:30
  94.7 20.9 %psum.7 = f32[16,450]{1,0:T(8,128)S(1)} all-reduce(f32[16,450]{1,0:T(8,128)S(1)} %bitcast_add_fusion), channel_id=1, replica_groups=mesh['lat'=32,'lon'=8,'lev'=4] {'lev'}, use_global_device_ids=true, to_apply=%region_2.3 | all-reduce | flops 7200 | bytes 57600 | tf_op jit(solution)/shard_map/psum | solution.py:150
  116.3 0.7 fusion.38
  (47 shorter events, 2.7 us)
Async XLA Ops:
  42.9 2.8 %copy-start = (f32[60,48,60]{2,0,1:T(8,128)}, f32[60,48,60]{2,0,1:T(8,128)S(1)}, u32[]{:S(2)}) copy-start(f32[60,48,60]{2,0,1:T(8,128)S(1)} %fusion.49) | copy-start | bytes 2073604
  45.7 1.6 %copy-start.7 = (s32[2,64]{1,0:T(2,128)S(1)}, s32[2,64]{1,0:T(2,128)}, u32[]{:S(2)}) copy-start(s32[2,64]{1,0:T(2,128)} %param.12) | copy-start | bytes 1540
  51.3 1.8 %copy-start.1 = (f32[60,48,60]{2,0,1:T(8,128)S(1)}, f32[60,48,60]{2,0,1:T(8,128)}, u32[]{:S(2)}) copy-start(f32[60,48,60]{2,0,1:T(8,128)} %copy-done) | copy-start | bytes 2073604
  62.9 1.1 copy-start.6
  62.9 1.2 copy-start.2
  62.9 31.6 %copy-start.8 = (f32[2]{0:T(128)S(1)}, f32[2]{0:T(128)}, u32[]{:S(2)}) copy-start(f32[2]{0:T(128)} %constant.83.clone) | copy-start | bytes 28
  62.9 53.3 %copy-start.3 = (f32[1,16,450]{2,1,0:T(8,128)S(1)}, f32[1,16,450]{2,1,0:T(8,128)}, u32[]{:S(2)}) copy-start(f32[1,16,450]{2,1,0:T(8,128)} %param.9) | copy-start | bytes 86404
  63.0 53.3 %copy-start.4 = (f32[1,16,450]{2,1,0:T(8,128)S(1)}, f32[1,16,450]{2,1,0:T(8,128)}, u32[]{:S(2)}) copy-start(f32[1,16,450]{2,1,0:T(8,128)} %param.8) | copy-start | bytes 86404
  63.0 53.3 %copy-start.5 = (f32[1,16,450]{2,1,0:T(8,128)S(1)}, f32[1,16,450]{2,1,0:T(8,128)}, u32[]{:S(2)}) copy-start(f32[1,16,450]{2,1,0:T(8,128)} %param.7) | copy-start | bytes 86404
  64.3 23.4 %collective-permute-start = (f32[3,1,16,1]{3,2,1,0:T(8,128)S(1)}, f32[3,1,16,1]{3,2,1,0:T(8,128)S(1)}, u32[]{:S(2)}, u32[]{:S(2)}) collective-permute-start(f32[3,1,16,1]{3,2,1,0:T(8,128)S(1)} %get-tuple-element.12), channel_id=1, source_target_pairs={{4,0},{8,4},{12,8},{16,12},{20,16},{24,20},{28,24},{0,28},{5,1},{9... | collective-permute-start | bytes 584 | tf_op jit(solution)/shard_map/ppermute | solution.py:22
  70.3 17.3 %collective-permute-start.1 = (f32[3,1,16,1]{3,2,1,0:T(8,128)S(1)}, f32[3,1,16,1]{3,2,1,0:T(8,128)S(1)}, u32[]{:S(2)}, u32[]{:S(2)}) collective-permute-start(f32[3,1,16,1]{3,2,1,0:T(8,128)S(1)} %get-tuple-element.13), channel_id=1, source_target_pairs={{0,4},{4,8},{8,12},{12,16},{16,20},{20,24},{24,28},{28,0},{1,5},{5... | collective-permute-start | bytes 584 | tf_op jit(solution)/shard_map/ppermute | solution.py:21
  72.3 15.5 %collective-permute-start.3 = (f32[2,1,1,450]{3,2,1,0:T(1,128)S(1)}, f32[2,1,1,450]{3,2,1,0:T(1,128)S(1)}, u32[]{:S(2)}, u32[]{:S(2)}) collective-permute-start(f32[2,1,1,450]{3,2,1,0:T(1,128)S(1)} %get-tuple-element.14), channel_id=1, source_target_pairs={{32,0},{64,32},{96,64},{128,96},{160,128},{192,160},{224,192},{256... | collective-permute-start | bytes 10808 | tf_op jit(solution)/shard_map/ppermute | solution.py:22
  75.6 12.2 %collective-permute-start.4 = (f32[2,1,1,450]{3,2,1,0:T(1,128)S(1)}, f32[2,1,1,450]{3,2,1,0:T(1,128)S(1)}, u32[]{:S(2)}, u32[]{:S(2)}) collective-permute-start(f32[2,1,1,450]{3,2,1,0:T(1,128)S(1)} %get-tuple-element.15), channel_id=1, source_target_pairs={{0,32},{32,64},{64,96},{96,128},{128,160},{160,192},{192,224},{224... | collective-permute-start | bytes 10808 | tf_op jit(solution)/shard_map/ppermute | solution.py:21
  80.3 14.3 %collective-permute-start.2 = (f32[2,1,2,450]{3,2,1,0:T(2,128)S(1)}, f32[2,1,2,450]{3,2,1,0:T(2,128)S(1)}, u32[]{:S(2)}, u32[]{:S(2)}) collective-permute-start(f32[2,1,2,450]{3,2,1,0:T(2,128)S(1)} %pad_maximum_fusion.14), channel_id=1, source_target_pairs={{0,16},{4,20},{8,24},{12,28},{16,0},{20,4},{24,8},{28,12},{1,17},{... | collective-permute-start | bytes 21608 | tf_op jit(solution)/shard_map/ppermute | solution.py:30
where the time goes:
time: 117 us
  blocking collectives  55.9 us (48%)
  starting transfers between devices  23.2 us (20%)
  matrix products  22.8 us (19%)
  waiting for transfers between devices  6.76 us (6%)
  local copies, waits for them, and re-layouts  4.23 us (4%)
  other arithmetic  3.21 us (3%)
    all_gather x1, blocking collectives, local(): circles = lax.all_gather(stacked, 'lon', axis=1, tiled=True)  34.9 us
    dot_general x12, matrix products, contract(): jnp.einsum(pattern, left_side, right_side, precision=lax.Precision.HIGHEST)  22.8 us
    psum x1, blocking collectives, local(): column_sum = lax.psum(jnp.sum(height_bar, axis=0), 'lev')  20.9 us
    ppermute x2, starting transfers between devices, with_halo(): after = lax.ppermute(initial, axis, down)  9.33 us
    ppermute x1, starting transfers between devices, shifted(): return lax.ppermute(value, axis, pairs)  7.22 us
    ppermute x1, waiting for transfers between devices, shifted(): return lax.ppermute(value, axis, pairs)  6.75 us
    ppermute x2, starting transfers between devices, with_halo(): before = lax.ppermute(last, axis, up)  6.61 us
  transfers between devices with their start and end apart: 5, of which 1 were waited for; matrix products, arithmetic and copies ran while one was open for 0% of the time, Pallas kernels for 0%

commit v1 on v0

v1 whole, which is shorter than its diff:
```python
import functools
import math

import jax
import jax.numpy as jnp
import ml_dtypes
import numpy as np
from jax import lax
from jax.experimental import pallas as pl
from jax.experimental.pallas import tpu as pltpu
from jax.sharding import PartitionSpec as P

zonal_courant = 0.15
merid_courant = 0.15
coriolis_scale = 0.4
heat_link_multiplier = 0.3

MESH = pl.DeviceIdType.MESH
PARTS = 8
ROOT_HALF = math.sqrt(0.5)


def lane_positions(width, padded):
    position = np.zeros(padded, np.int64)
    position[:width] = np.arange(width)
    position[width] = width
    position[padded - 1] = -1
    used = np.zeros(padded, bool)
    used[: width + 1] = True
    used[padded - 1] = True
    return position, used


def wave_tables(width, padded):
    position, used = lane_positions(width, padded)
    index = np.arange(padded)
    angle = 2.0 * np.pi * ((index[:, None] * position[None, :]) % width) / width
    live = (index < width)[:, None] & used[None, :]
    both = np.concatenate([np.where(live, np.cos(angle), 0.0), np.where(live, np.sin(angle), 0.0)], axis=1)
    high = both.astype(np.float32).astype(ml_dtypes.bfloat16)
    low = (both - high.astype(np.float64)).astype(np.float32).astype(ml_dtypes.bfloat16)
    residue = np.arange(8)
    twist = 2.0 * np.pi * ((residue[:, None] * position[None, :]) % (width * PARTS)) / (width * PARTS)
    twists = np.stack([np.cos(twist), np.sin(twist)]).astype(np.float32)
    return np.stack([high, low]), twists


def split(value):
    high = value.astype(jnp.bfloat16)
    return high, (value - high.astype(jnp.float32)).astype(jnp.bfloat16)


def wave_product(stack_ref, table_ref):
    rows = stack_ref.shape[0]
    high, low = split(stack_ref[...])
    lead = jnp.dot(jnp.concatenate([high, low], axis=0), table_ref[0], preferred_element_type=jnp.float32)
    rest = jnp.dot(high, table_ref[1], preferred_element_type=jnp.float32)
    return lead[:rows] + lead[rows:] + rest


def filter_blocks(blocks, result, stack, table, twists, cuts, width):
    rows, lanes = blocks.shape[1:]
    x = [blocks[d] for d in range(PARTS)]
    a = [x[d] + x[d + 4] for d in range(4)]
    b = [x[d] - x[d + 4] for d in range(4)]
    b_minus = (b[1] - b[3]) * ROOT_HALF
    b_plus = (b[1] + b[3]) * ROOT_HALF
    even, odd = a[0] + a[2], a[1] + a[3]
    waves = [
        (even + odd, None),
        (b[0] + b_minus, -b[2] - b_plus),
        (a[0] - a[2], a[3] - a[1]),
        (b[0] - b_minus, b[2] - b_plus),
        (even - odd, None),
    ]
    for r, (re, im) in enumerate(waves):
        if r == 0:
            new_re, new_im = re, jnp.zeros_like(re)
        else:
            c, s = twists[0, r : r + 1, :], twists[1, r : r + 1, :]
            new_re = re * c if im is None else re * c + im * s
            new_im = -re * s if im is None else im * c - re * s
        stack[8 * r : 8 * r + rows, :] = new_re
        stack[40 + 8 * r : 40 + 8 * r + rows, :] = new_im
    first = wave_product(stack, table)
    q = lax.broadcasted_iota(jnp.int32, (8, lanes), 1)
    row = lax.broadcasted_iota(jnp.int32, (8, lanes), 0)
    cut = jnp.where(lax.rem(row, 2) == 0, cuts[0], cuts[1])
    for r in range(5):
        wave = PARTS * q + r
        wave = jnp.minimum(wave, PARTS * width - wave).astype(jnp.float32)
        ratio = cut / jnp.maximum(wave, 1.0)
        weight = (1.0 if r in (0, 4) else 2.0) / (PARTS * width)
        factor = jnp.where(wave <= cut, 1.0, ratio * ratio) * weight
        factor = jnp.where(q < width, factor, 0.0)
        lo, hi = 8 * r, 40 + 8 * r
        re = first[lo : lo + 8, :lanes] + first[hi : hi + 8, lanes:]
        im = first[hi : hi + 8, :lanes] - first[lo : lo + 8, lanes:]
        stack[lo : lo + 8, :] = re * factor
        stack[hi : hi + 8, :] = im * factor
    second = wave_product(stack, table)
    back = []
    for r in range(5):
        lo, hi = 8 * r, 40 + 8 * r
        re = second[lo : lo + 8, :lanes] - second[hi : hi + 8, lanes:]
        if r == 0:
            back.append((re, None))
            continue
        im = second[hi : hi + 8, :lanes] + second[lo : lo + 8, lanes:]
        c, s = twists[0, r : r + 1, :], twists[1, r : r + 1, :]
        back.append((re * c - im * s, None if r == 4 else im * c + re * s))
    r0, r4 = back[0][0], back[4][0]
    (r1, i1), (r2, i2), (r3, i3) = back[1], back[2], back[3]
    plus, minus = r0 + r4, r0 - r4
    even_a, even_b = plus + r2, plus - r2
    odd_a, odd_b = minus - i2, minus + i2
    half = [
        r1 + r3,
        ((r1 - r3) - (i1 + i3)) * ROOT_HALF,
        i3 - i1,
        ((r3 - r1) - (i1 + i3)) * ROOT_HALF,
    ]
    base = [even_a, odd_a, even_b, odd_b]
    for d in range(4):
        result[d] = (base[d] + half[d])[:rows]
        result[d + 4] = (base[d] - half[d])[:rows]


def kernel(sizes, u_ref, v_ref, t_ref, p_ref, g_ref, cut_ref, table_hbm, twists,
           out_u, out_v, out_t, out_p,
           table, raw, pack, circles, stack, filtered, home, smooth,
           edge_out, edge_in, row_out, row_in, ghost, ext, height, heights,
           table_sem, edge_send, edge_recv, row_send, row_recv, circ_send, circ_recv,
           home_send, home_recv, ghost_send, ghost_recv, lev_send, lev_recv):
    lats, lons, levs, polar_ranks = sizes
    rows, width = p_ref.shape
    lanes = raw.shape[-1]
    lat, lon, lev = lax.axis_index("lat"), lax.axis_index("lon"), lax.axis_index("lev")
    polar_lat = lambda r: (r < polar_ranks) | (r >= lats - polar_ranks)
    polar = polar_lat(lat)
    across = lax.rem(lon + PARTS // 2, PARTS)
    south_filtered = (lat == 0) | polar_lat(lat - 1)
    north_filtered = (lat == lats - 1) | polar_lat(lat + 1)

    table_copy = pltpu.make_async_copy(table_hbm, table, table_sem)

    @pl.when(polar)
    def _():
        table_copy.start()

    barrier = pltpu.get_barrier_semaphore()

    def greet(**where):
        pl.semaphore_signal(barrier, inc=1, device_id=where, device_id_type=MESH)

    for k in range(1, PARTS):
        greet(lon=lax.rem(lon + k, PARTS))
    for k in range(1, levs):
        greet(lev=lax.rem(lev + k, levs))

    @pl.when(lat > 0)
    def _():
        greet(lat=lat - 1)

        @pl.when(south_filtered & (lon != PARTS - 1))
        def _():
            greet(lat=lat - 1, lon=PARTS - 1)

    @pl.when(lat < lats - 1)
    def _():
        greet(lat=lat + 1)

        @pl.when(north_filtered & (lon != 0))
        def _():
            greet(lat=lat + 1, lon=0)

    lane = lax.broadcasted_iota(jnp.int32, (rows, lanes), 1)
    last_tile = (width // 128) * 128
    for f, ref in enumerate((u_ref, v_ref, t_ref, g_ref, p_ref)):
        raw[f, :, last_tile:] = jnp.zeros((rows, lanes - last_tile), jnp.float32)
        raw[f, :, :width] = ref[...] if f == 4 else ref[0]
    raw_u, raw_v, raw_t, raw_g, raw_p = (raw[f] for f in range(5))
    small = lax.broadcasted_iota(jnp.int32, (rows, 128), 1)
    for side, column in ((0, 0), (1, width - 1)):
        edge = jnp.zeros((rows, 128), jnp.float32)
        for f, value in enumerate((raw_u, raw_t, raw_g, raw_p)):
            edge = jnp.where(small == f, value[:, column : column + 1], edge)
        edge_out[side] = edge
    for side, row in ((0, 0), (1, rows - 1)):
        for f, value in enumerate((raw_v, raw_t, raw_p)):
            row_out[side, f : f + 1, :] = value[row : row + 1]

    @pl.when(polar)
    def _():
        for e in range(PARTS):
            for f, value in enumerate((raw_u, raw_v, raw_t)):
                pack[e, 2 * f : 2 * f + 2, :] = value[2 * e : 2 * e + 2]

    count = lambda condition: jnp.where(condition, 1, 0)
    below, above = lat > 0, lat < lats - 1
    arrivals = PARTS - 1 + levs - 1 + count(below) + count(above)
    arrivals += (PARTS - 1) * count(polar & ((below & (lon == 0)) | (above & (lon == PARTS - 1))))
    pl.semaphore_wait(barrier, arrivals)

    def send(src, dst, send_sem, recv_sem, **where):
        return pltpu.make_async_remote_copy(
            src_ref=src, dst_ref=dst, send_sem=send_sem, recv_sem=recv_sem,
            device_id=where, device_id_type=MESH)

    circ_copies = [
        send(pack.at[lax.rem(lon + k, PARTS)], circles.at[lon], circ_send.at[k], circ_recv.at[k],
             lon=lax.rem(lon + k, PARTS))
        for k in range(1, PARTS)
    ]

    @pl.when(polar)
    def _():
        for k in (4, 3, 5, 2, 6, 1, 7):
            circ_copies[k - 1].start()

    edge_copies = [
        send(edge_out.at[0], edge_in.at[0], edge_send.at[0], edge_recv.at[0], lon=lax.rem(lon + PARTS - 1, PARTS)),
        send(edge_out.at[1], edge_in.at[1], edge_send.at[1], edge_recv.at[1], lon=lax.rem(lon + 1, PARTS)),
    ]
    for copy in edge_copies:
        copy.start()

    @pl.when(lat > 0)
    def _():
        send(row_out.at[0], row_in.at[1], row_send.at[0], row_recv.at[1], lat=lat - 1).start()

    @pl.when(lat == 0)
    def _():
        send(row_out.at[0], row_in.at[0], row_send.at[0], row_recv.at[0], lon=across).start()

    @pl.when(lat < lats - 1)
    def _():
        send(row_out.at[1], row_in.at[0], row_send.at[1], row_recv.at[0], lat=lat + 1).start()

    @pl.when(lat == lats - 1)
    def _():
        send(row_out.at[1], row_in.at[1], row_send.at[1], row_recv.at[1], lon=across).start()

    @pl.when(polar)
    def _():
        own = jnp.where(lat < polar_ranks, 0, 1)
        row = lat * rows + 2 * lon
        cuts = []
        for j in range(2):
            rank = jnp.where(own == 0, row + j, lats * rows - 1 - (row + j))
            cuts.append(cut_ref[own, rank].astype(jnp.float32))
        circles[lon] = pack[lon]
        table_copy.wait()
        for k in range(1, PARTS):
            circ_copies[k - 1].wait_recv()
        filter_blocks(circles, filtered, stack, table, twists, cuts, width)

    home_copies = [
        send(filtered.at[lax.rem(lon + k, PARTS)], home.at[lon], home_send.at[k], home_recv.at[k],
             lon=lax.rem(lon + k, PARTS))
        for k in range(1, PARTS)
    ]

    def ghost_copy(d, side, **where):
        return send(filtered.at[d], ghost.at[side], ghost_send.at[d], ghost_recv.at[side], **where)

    def ghost_copies(act):
        @pl.when(polar & (lon == 0))
        def _():
            for d in range(PARTS):
                @pl.when(lat > 0)
                def _():
                    act(ghost_copy(d, 1, lat=lat - 1, lon=d))

                if d != PARTS // 2:
                    @pl.when(lat == 0)
                    def _():
                        act(ghost_copy(d, 0, lon=(d + PARTS // 2) % PARTS))

        @pl.when(polar & (lon == PARTS - 1))
        def _():
            for d in range(PARTS):
                @pl.when(lat < lats - 1)
                def _():
                    act(ghost_copy(d, 0, lat=lat + 1, lon=d))

                if d != PARTS // 2 - 1:
                    @pl.when(lat == lats - 1)
                    def _():
                        act(ghost_copy(d, 1, lon=(d + PARTS // 2) % PARTS))

    self_south = (lat == 0) & (lon == 0)
    self_north = (lat == lats - 1) & (lon == PARTS - 1)

    @pl.when(polar)
    def _():
        for k in (4, 3, 5, 2, 6, 1, 7):
            home_copies[k - 1].start()

    ghost_copies(lambda copy: copy.start())

    @pl.when(self_south)
    def _():
        ghost[0] = filtered[PARTS // 2]

    @pl.when(self_north)
    def _():
        ghost[1] = filtered[PARTS // 2 - 1]

    for copy in edge_copies:
        copy.wait_recv()
    for side in range(2):
        pltpu.make_async_copy(row_out.at[side], row_in.at[side], row_recv.at[side]).wait()

    def with_edges(value, f):
        east, west = edge_in[0][:, f : f + 1], edge_in[1][:, f : f + 1]
        return jnp.where(lane == width, east, jnp.where(lane == lanes - 1, west, value))

    flow, pres = with_edges(raw_g, 2), with_edges(raw_p, 3)

    @pl.when(jnp.logical_not(polar))
    def _():
        smooth[0] = with_edges(raw_u, 0)
        smooth[1] = raw_v
        smooth[2] = with_edges(raw_t, 1)

    latitude = (lat * rows + lax.broadcasted_iota(jnp.int32, (rows, 128), 0)).astype(jnp.float32)
    latitude = ((latitude + 0.5) / (lats * rows) - 0.5) * jnp.float32(math.pi)
    scale = (zonal_courant / jnp.cos(latitude))[:, :1]
    coriolis = (coriolis_scale * jnp.sin(latitude))[:, :1]

    @pl.when(polar)
    def _():
        home[lon] = filtered[lon]
        for k in range(1, PARTS):
            home_copies[k - 1].wait_recv()
        for e in range(PARTS):
            for f in range(3):
                smooth[f, 2 * e : 2 * e + 2, :] = home[e, 2 * f : 2 * f + 2, :]

    @pl.when(south_filtered & jnp.logical_not(self_south))
    def _():
        pltpu.make_async_copy(filtered.at[0], ghost.at[0], ghost_recv.at[0]).wait()

    @pl.when(north_filtered & jnp.logical_not(self_north))
    def _():
        pltpu.make_async_copy(filtered.at[0], ghost.at[1], ghost_recv.at[1]).wait()

    def zonal(value):
        return pltpu.roll(value, lanes - 1, 1) - pltpu.roll(value, 1, 1)

    fu, fv, ft = smooth[0], smooth[1], smooth[2]
    div = -heat_link_multiplier * ft - pres * (1.0 / levs)
    ext[0, 8 : 8 + rows, :] = fv
    ext[1, 8 : 8 + rows, :] = div
    for side, at in ((0, 7), (1, 8 + rows)):
        wanted = south_filtered if side == 0 else north_filtered
        pole = (lat == 0) if side == 0 else (lat == lats - 1)
        upper = jnp.where(pole, side == 1, side == 0)
        g = ghost[side]
        gv = jnp.where(upper, g[3:4], g[2:3])
        gt = jnp.where(upper, g[5:6], g[4:5])
        gv = jnp.where(wanted, gv, row_in[side, 0:1, :])
        gt = jnp.where(wanted, gt, row_in[side, 1:2, :])
        gp = row_in[side, 2:3, :]
        ext[0, at : at + 1, :] = jnp.where(pole, -gv, gv)
        ext[1, at : at + 1, :] = -heat_link_multiplier * gt - gp * (1.0 / levs)
    merid_v = ext[0, 9 : 9 + rows, :] - ext[0, 7 : 7 + rows, :]
    merid_div = ext[1, 9 : 9 + rows, :] - ext[1, 7 : 7 + rows, :]
    bar = scale * zonal(fu) + merid_courant * merid_v
    height[...] = bar
    lev_copies = [
        send(height, heights.at[k], lev_send.at[k], lev_recv.at[k], lev=lax.rem(lev + k, levs))
        for k in range(1, levs)
    ]
    for copy in lev_copies:
        copy.start()
    out_u[0] = (raw_u - coriolis * fv - scale * zonal(div))[:, :width]
    out_v[0] = (raw_v + coriolis * fu - merid_courant * merid_div)[:, :width]
    out_t[0] = (raw_t + bar + scale * zonal(flow * ft))[:, :width]

    for copy in edge_copies:
        copy.wait_send()
    for side in range(2):
        pltpu.make_async_copy(row_out.at[side], row_in.at[side], row_send.at[side]).wait()

    @pl.when(polar)
    def _():
        for copy in circ_copies:
            copy.wait_send()
        for copy in home_copies:
            copy.wait_send()

    ghost_copies(lambda copy: copy.wait_send())
    total = raw_p + bar
    for copy in lev_copies:
        copy.wait_recv()
    for k in range(1, levs):
        total = total + heights[k]
    out_p[...] = total[:, :width]
    for copy in lev_copies:
        copy.wait_send()


def solution(mesh):
    lats, lons, levs = mesh.shape["lat"], mesh.shape["lon"], mesh.shape["lev"]
    field, plane = P("lev", "lat", "lon"), P("lat", "lon")

    def local(adjoint_u, adjoint_v, adjoint_temp, adjoint_pres, carrying_eastward_flow, cutoff):
        rows, width = adjoint_pres.shape
        lanes = (width + 2 + 127) // 128 * 128
        table, twists = wave_tables(width, lanes)
        sizes = (lats, lons, levs, cutoff.shape[1] // rows)
        vmem = pl.BlockSpec(memory_space=pltpu.VMEM)
        f32, dma = jnp.float32, pltpu.SemaphoreType.DMA
        block = (PARTS, 6, lanes)
        return pl.pallas_call(
            functools.partial(kernel, sizes),
            name="adjoint_step",
            out_shape=[jax.ShapeDtypeStruct(adjoint_u.shape, f32)] * 3
            + [jax.ShapeDtypeStruct(adjoint_pres.shape, f32)],
            in_specs=[vmem] * 5
            + [pl.BlockSpec(memory_space=pltpu.SMEM), pl.BlockSpec(memory_space=pl.ANY), vmem],
            out_specs=[vmem] * 4,
            scratch_shapes=[
                pltpu.VMEM(table.shape, jnp.bfloat16),
                pltpu.VMEM((5, rows, lanes), f32),
                pltpu.VMEM(block, f32),
                pltpu.VMEM(block, f32),
                pltpu.VMEM((80, lanes), f32),
                pltpu.VMEM(block, f32),
                pltpu.VMEM(block, f32),
                pltpu.VMEM((3, rows, lanes), f32),
                pltpu.VMEM((2, rows, 128), f32),
                pltpu.VMEM((2, rows, 128), f32),
                pltpu.VMEM((2, 3, lanes), f32),
                pltpu.VMEM((2, 3, lanes), f32),
                pltpu.VMEM((2, 6, lanes), f32),
                pltpu.VMEM((2, rows + 16, lanes), f32),
                pltpu.VMEM((rows, lanes), f32),
                pltpu.VMEM((levs, rows, lanes), f32),
                dma, dma((2,)), dma((2,)), dma((2,)), dma((2,)),
                dma((PARTS,)), dma((PARTS,)), dma((PARTS,)), dma((PARTS,)),
                dma((PARTS,)), dma((2,)), dma((levs,)), dma((levs,)),
            ],
            compiler_params=pltpu.CompilerParams(collective_id=0, has_side_effects=True),
        )(adjoint_u, adjoint_v, adjoint_temp, adjoint_pres, carrying_eastward_flow, cutoff,
          jnp.asarray(table), jnp.asarray(twists))

    return jax.shard_map(
        local, mesh=mesh, in_specs=(field, field, field, plane, field, P()),
        out_specs=(field, field, field, plane), check_vma=False)
```

time: 117 us -> 55.1 us (0.47)
  the two profiles are of different devices: /device:TPU:58 before, /device:TPU:62 now
where the time goes in v1:
time: 55.1 us; the launch traced here: 54.6 us
  Pallas kernels  48.5 us (88%)
  local copies, waits for them, and re-layouts  5.5 us (10%)
  between operations  0.64 us (1%)
    pallas_call x1, Pallas kernels, local(): pl.pallas_call(functools.partial(kernel, sizes), name='adjoint_step', out...  48.5 us
    unnamed x4, local copies, waits for them, and re-layouts  5.5 us

profile of v1, /device:TPU:62, one launch (start us, length us, event | category | flops | bytes accessed | tf_op | source)
XLA Modules:
  0.0 54.6 jit_solution(7825920845987156682)
XLA Ops:
  0.6 48.5 %adjoint_step.1 = (f32[1,16,450]{2,1,0:T(8,128)}, f32[1,16,450]{2,1,0:T(8,128)}, f32[1,16,450]{2,1,0:T(8,128)}, f32[16,450]{1,0:T(8,128)}) custom-call(f32[1,16,450]{2,1,0:T(8,128)} %u_ref.1, f32[1,16,450]{2,1,0:T(8,128)} %v_ref.1, f32[1,16,450]{2,1,0:T(8,128)} %t_ref.1, f32[16,450]{1,0:T(8,128)} %p_ref.1, f32[1,16,450]{2,1,0:T(8,128)} %g_ref.1, ...), custom_call_target="tpu_custom_call" | custom-call | tf_op jit(solution)/shard_map/adjoint_step/pallas_call | solution.py:417
  49.1 1.4 %copy.16 = f32[1,16,450]{2,1,0:T(8,128)} copy(f32[1,16,450]{2,1,0:T(8,128)} %get-tuple-element.8) | data formatting | bytes 57600
  50.5 1.4 %copy.17 = f32[1,16,450]{2,1,0:T(8,128)} copy(f32[1,16,450]{2,1,0:T(8,128)} %get-tuple-element.9) | data formatting | bytes 57600
  51.9 1.4 %copy.18 = f32[1,16,450]{2,1,0:T(8,128)} copy(f32[1,16,450]{2,1,0:T(8,128)} %get-tuple-element.10) | data formatting | bytes 57600
  53.3 1.4 %copy.19 = f32[16,450]{1,0:T(8,128)} copy(f32[16,450]{1,0:T(8,128)} %get-tuple-element.11) | data formatting | bytes 57600

commit v2 on v1

--- a/solution.py
+++ b/solution.py
@@ -126,11 +126,10 @@
         result[d + 4] = (base[d] - half[d])[:rows]
 
 
-def kernel(sizes, u_ref, v_ref, t_ref, p_ref, g_ref, cut_ref, table_hbm, twists,
-           out_u, out_v, out_t, out_p,
-           table, raw, pack, circles, stack, filtered, home, smooth,
-           edge_out, edge_in, row_out, row_in, ghost, ext, height, heights,
-           table_sem, edge_send, edge_recv, row_send, row_recv, circ_send, circ_recv,
+def kernel(sizes, u_hbm, v_hbm, t_hbm, p_hbm, g_hbm, cut_ref, table_hbm, twists_hbm, packed,
+           u_ref, v_ref, t_ref, p_ref, g_ref, twists, table, raw, pack, circles, stack, filtered, home, smooth,
+           edge_out, edge_in, row_out, row_in, ghost_out, ghost, ext, height, heights,
+           input_sem, table_sem, edge_send, edge_recv, row_send, row_recv, circ_send, circ_recv,
            home_send, home_recv, ghost_send, ghost_recv, lev_send, lev_recv):
     lats, lons, levs, polar_ranks = sizes
     rows, width = p_ref.shape
@@ -142,12 +141,6 @@
     south_filtered = (lat == 0) | polar_lat(lat - 1)
     north_filtered = (lat == lats - 1) | polar_lat(lat + 1)
 
-    table_copy = pltpu.make_async_copy(table_hbm, table, table_sem)
-
-    @pl.when(polar)
-    def _():
-        table_copy.start()
-
     barrier = pltpu.get_barrier_semaphore()
 
     def greet(**where):
@@ -174,9 +167,27 @@
         def _():
             greet(lat=lat + 1, lon=0)
 
+    input_copies = [
+        pltpu.make_async_copy(src, dst, input_sem.at[k])
+        for k, (src, dst) in enumerate(
+            ((u_hbm, u_ref), (v_hbm, v_ref), (t_hbm, t_ref), (g_hbm, g_ref), (p_hbm, p_ref)))
+    ]
+    table_copies = [
+        pltpu.make_async_copy(twists_hbm, twists, table_sem.at[0]),
+        pltpu.make_async_copy(table_hbm, table, table_sem.at[1]),
+    ]
+    for copy in input_copies:
+        copy.start()
+
+    @pl.when(polar)
+    def _():
+        for copy in table_copies:
+            copy.start()
+
     lane = lax.broadcasted_iota(jnp.int32, (rows, lanes), 1)
     last_tile = (width // 128) * 128
     for f, ref in enumerate((u_ref, v_ref, t_ref, g_ref, p_ref)):
+        input_copies[f].wait()
         raw[f, :, last_tile:] = jnp.zeros((rows, lanes - last_tile), jnp.float32)
         raw[f, :, :width] = ref[...] if f == 4 else ref[0]
     raw_u, raw_v, raw_t, raw_g, raw_p = (raw[f] for f in range(5))
@@ -250,7 +261,8 @@
             rank = jnp.where(own == 0, row + j, lats * rows - 1 - (row + j))
             cuts.append(cut_ref[own, rank].astype(jnp.float32))
         circles[lon] = pack[lon]
-        table_copy.wait()
+        for copy in table_copies:
+            copy.wait()
         for k in range(1, PARTS):
             circ_copies[k - 1].wait_recv()
         filter_blocks(circles, filtered, stack, table, twists, cuts, width)
@@ -262,7 +274,7 @@
     ]
 
     def ghost_copy(d, side, **where):
-        return send(filtered.at[d], ghost.at[side], ghost_send.at[d], ghost_recv.at[side], **where)
+        return send(ghost_out.at[d], ghost.at[side], ghost_send.at[d], ghost_recv.at[side], **where)
 
     def ghost_copies(act):
         @pl.when(polar & (lon == 0))
@@ -289,6 +301,18 @@
                     def _():
                         act(ghost_copy(d, 1, lon=(d + PARTS // 2) % PARTS))
 
+    @pl.when(polar & (lon == 0))
+    def _():
+        for d in range(PARTS):
+            ghost_out[d, 0:1, :] = filtered[d, 2:3, :]
+            ghost_out[d, 1:2, :] = filtered[d, 4:5, :]
+
+    @pl.when(polar & (lon == PARTS - 1))
+    def _():
+        for d in range(PARTS):
+            ghost_out[d, 0:1, :] = filtered[d, 3:4, :]
+            ghost_out[d, 1:2, :] = filtered[d, 5:6, :]
+
     self_south = (lat == 0) & (lon == 0)
     self_north = (lat == lats - 1) & (lon == PARTS - 1)
 
@@ -301,11 +325,11 @@
 
     @pl.when(self_south)
     def _():
-        ghost[0] = filtered[PARTS // 2]
+        ghost[0] = ghost_out[PARTS // 2]
 
     @pl.when(self_north)
     def _():
-        ghost[1] = filtered[PARTS // 2 - 1]
+        ghost[1] = ghost_out[PARTS // 2 - 1]
 
     for copy in edge_copies:
         copy.wait_recv()
@@ -340,11 +364,11 @@
 
     @pl.when(south_filtered & jnp.logical_not(self_south))
     def _():
-        pltpu.make_async_copy(filtered.at[0], ghost.at[0], ghost_recv.at[0]).wait()
+        pltpu.make_async_copy(ghost_out.at[0], ghost.at[0], ghost_recv.at[0]).wait()
 
     @pl.when(north_filtered & jnp.logical_not(self_north))
     def _():
-        pltpu.make_async_copy(filtered.at[0], ghost.at[1], ghost_recv.at[1]).wait()
+        pltpu.make_async_copy(ghost_out.at[0], ghost.at[1], ghost_recv.at[1]).wait()
 
     def zonal(value):
         return pltpu.roll(value, lanes - 1, 1) - pltpu.roll(value, 1, 1)
@@ -356,12 +380,8 @@
     for side, at in ((0, 7), (1, 8 + rows)):
         wanted = south_filtered if side == 0 else north_filtered
         pole = (lat == 0) if side == 0 else (lat == lats - 1)
-        upper = jnp.where(pole, side == 1, side == 0)
-        g = ghost[side]
-        gv = jnp.where(upper, g[3:4], g[2:3])
-        gt = jnp.where(upper, g[5:6], g[4:5])
-        gv = jnp.where(wanted, gv, row_in[side, 0:1, :])
-        gt = jnp.where(wanted, gt, row_in[side, 1:2, :])
+        gv = jnp.where(wanted, ghost[side, 0:1, :], row_in[side, 0:1, :])
+        gt = jnp.where(wanted, ghost[side, 1:2, :], row_in[side, 1:2, :])
         gp = row_in[side, 2:3, :]
         ext[0, at : at + 1, :] = jnp.where(pole, -gv, gv)
         ext[1, at : at + 1, :] = -heat_link_multiplier * gt - gp * (1.0 / levs)
@@ -375,9 +395,9 @@
     ]
     for copy in lev_copies:
         copy.start()
-    out_u[0] = (raw_u - coriolis * fv - scale * zonal(div))[:, :width]
-    out_v[0] = (raw_v + coriolis * fu - merid_courant * merid_div)[:, :width]
-    out_t[0] = (raw_t + bar + scale * zonal(flow * ft))[:, :width]
+    packed[0] = (raw_u - coriolis * fv - scale * zonal(div))
+    packed[1] = (raw_v + coriolis * fu - merid_courant * merid_div)
+    packed[2] = (raw_t + bar + scale * zonal(flow * ft))
 
     for copy in edge_copies:
         copy.wait_send()
@@ -397,9 +417,17 @@
         copy.wait_recv()
     for k in range(1, levs):
         total = total + heights[k]
-    out_p[...] = total[:, :width]
+    packed[3] = total
     for copy in lev_copies:
         copy.wait_send()
+
+
+def unpack(packed, out_u, out_v, out_t, out_p):
+    width = out_p.shape[-1]
+    out_u[0] = packed[0, :, :width]
+    out_v[0] = packed[1, :, :width]
+    out_t[0] = packed[2, :, :width]
+    out_p[...] = packed[3, :, :width]
 
 
 def solution(mesh):
@@ -412,17 +440,22 @@
         table, twists = wave_tables(width, lanes)
         sizes = (lats, lons, levs, cutoff.shape[1] // rows)
         vmem = pl.BlockSpec(memory_space=pltpu.VMEM)
+        anywhere = pl.BlockSpec(memory_space=pl.ANY)
         f32, dma = jnp.float32, pltpu.SemaphoreType.DMA
         block = (PARTS, 6, lanes)
-        return pl.pallas_call(
+        packed = pl.pallas_call(
             functools.partial(kernel, sizes),
             name="adjoint_step",
-            out_shape=[jax.ShapeDtypeStruct(adjoint_u.shape, f32)] * 3
-            + [jax.ShapeDtypeStruct(adjoint_pres.shape, f32)],
-            in_specs=[vmem] * 5
-            + [pl.BlockSpec(memory_space=pltpu.SMEM), pl.BlockSpec(memory_space=pl.ANY), vmem],
-            out_specs=[vmem] * 4,
+            out_shape=jax.ShapeDtypeStruct((4, rows, lanes), f32),
+            in_specs=[anywhere] * 5 + [pl.BlockSpec(memory_space=pltpu.SMEM)] + [anywhere] * 2,
+            out_specs=vmem,
             scratch_shapes=[
+                pltpu.VMEM((1, rows, width), f32),
+                pltpu.VMEM((1, rows, width), f32),
+                pltpu.VMEM((1, rows, width), f32),
+                pltpu.VMEM((rows, width), f32),
+                pltpu.VMEM((1, rows, width), f32),
+                pltpu.VMEM(twists.shape, f32),
                 pltpu.VMEM(table.shape, jnp.bfloat16),
                 pltpu.VMEM((5, rows, lanes), f32),
                 pltpu.VMEM(block, f32),
@@ -435,17 +468,26 @@
                 pltpu.VMEM((2, rows, 128), f32),
                 pltpu.VMEM((2, 3, lanes), f32),
                 pltpu.VMEM((2, 3, lanes), f32),
-                pltpu.VMEM((2, 6, lanes), f32),
+                pltpu.VMEM((PARTS, 2, lanes), f32),
+                pltpu.VMEM((2, 2, lanes), f32),
                 pltpu.VMEM((2, rows + 16, lanes), f32),
                 pltpu.VMEM((rows, lanes), f32),
                 pltpu.VMEM((levs, rows, lanes), f32),
-                dma, dma((2,)), dma((2,)), dma((2,)), dma((2,)),
+                dma((5,)), dma((2,)), dma((2,)), dma((2,)), dma((2,)), dma((2,)),
                 dma((PARTS,)), dma((PARTS,)), dma((PARTS,)), dma((PARTS,)),
                 dma((PARTS,)), dma((2,)), dma((levs,)), dma((levs,)),
             ],
             compiler_params=pltpu.CompilerParams(collective_id=0, has_side_effects=True),
         )(adjoint_u, adjoint_v, adjoint_temp, adjoint_pres, carrying_eastward_flow, cutoff,
           jnp.asarray(table), jnp.asarray(twists))
+        return pl.pallas_call(
+            unpack,
+            name="hand_on",
+            out_shape=[jax.ShapeDtypeStruct(adjoint_u.shape, f32)] * 3
+            + [jax.ShapeDtypeStruct(adjoint_pres.shape, f32)],
+            in_specs=[vmem],
+            out_specs=[vmem] * 4,
+        )(packed)
 
     return jax.shard_map(
         local, mesh=mesh, in_specs=(field, field, field, plane, field, P()),

time: 55.1 us -> 49.6 us (0.900)
  the two profiles are of different devices: /device:TPU:62 before, /device:TPU:24 now
where the time goes in v2:
time: 49.6 us; the launch traced here: 49.4 us
  Pallas kernels  48.8 us (98%)
  between operations  0.64 us (1%)
    pallas_call x1, Pallas kernels, local(): pl.pallas_call(functools.partial(kernel, sizes), name='adjoint_step', out...  47.2 us
    pallas_call x1, Pallas kernels, local(): pl.pallas_call(unpack, name='hand_on', out_shape=[jax.ShapeDtypeStruct(ad...  1.56 us

profile of v2, /device:TPU:24, one launch (start us, length us, event | category | flops | bytes accessed | tf_op | source)
XLA Modules:
  0.0 49.4 jit_solution(2130904247683150212)
XLA Ops:
  0.6 47.2 %adjoint_step.1.packed = f32[4,16,512]{2,1,0:T(8,128)} custom-call(f32[1,16,450]{2,1,0:T(8,128)} %u_hbm.1, f32[1,16,450]{2,1,0:T(8,128)} %v_hbm.1, f32[1,16,450]{2,1,0:T(8,128)} %t_hbm.1, f32[16,450]{1,0:T(8,128)} %p_hbm.1, f32[1,16,450]{2,1,0:T(8,128)} %g_hbm.1, s32[2,64]{1,0:T(2,128)} %cut_ref.1, bf16[2,512,1024]{2,1,0:T(8,128)(2,1)} %constant.4.clone.table_hbm, ...), custom_call_target="tpu_custom_call" | custom-call | tf_op jit(solution)/shard_map/adjoint_step/pallas_call | solution.py:446
  47.9 1.6 %hand_on.1 = (f32[1,16,450]{2,1,0:T(8,128)}, f32[1,16,450]{2,1,0:T(8,128)}, f32[1,16,450]{2,1,0:T(8,128)}, f32[16,450]{1,0:T(8,128)}) custom-call(f32[4,16,512]{2,1,0:T(8,128)} %adjoint_step.1.packed), custom_call_target="tpu_custom_call" | custom-call | tf_op jit(solution)/shard_map/hand_on/pallas_call | solution.py:483

commit v3 on v2

--- a/solution.py
+++ b/solution.py
@@ -128,8 +128,8 @@
 
 def kernel(sizes, u_hbm, v_hbm, t_hbm, p_hbm, g_hbm, cut_ref, table_hbm, twists_hbm, packed,
            u_ref, v_ref, t_ref, p_ref, g_ref, twists, table, raw, pack, circles, stack, filtered, home, smooth,
-           edge_out, edge_in, row_out, row_in, ghost_out, ghost, ext, height, heights,
-           input_sem, table_sem, edge_send, edge_recv, row_send, row_recv, circ_send, circ_recv,
+           edge_out, edge_in, row_out, row_in, pole_in, ghost_out, ghost, ext, height, heights,
+           input_sem, table_sem, edge_send, edge_recv, row_send, row_recv, pole_recv, circ_send, circ_recv,
            home_send, home_recv, ghost_send, ghost_recv, lev_send, lev_recv):
     lats, lons, levs, polar_ranks = sizes
     rows, width = p_ref.shape
@@ -137,7 +137,7 @@
     lat, lon, lev = lax.axis_index("lat"), lax.axis_index("lon"), lax.axis_index("lev")
     polar_lat = lambda r: (r < polar_ranks) | (r >= lats - polar_ranks)
     polar = polar_lat(lat)
-    across = lax.rem(lon + PARTS // 2, PARTS)
+    far = lax.rem(lev + levs // 2, levs)
     south_filtered = (lat == 0) | polar_lat(lat - 1)
     north_filtered = (lat == lats - 1) | polar_lat(lat + 1)
 
@@ -146,26 +146,29 @@
     def greet(**where):
         pl.semaphore_signal(barrier, inc=1, device_id=where, device_id_type=MESH)
 
-    for k in range(1, PARTS):
-        greet(lon=lax.rem(lon + k, PARTS))
+    for k in range(PARTS):
+        greet(lon=lax.rem(lon + k, PARTS), lev=far)
+    greet(lon=lax.rem(lon + 1, PARTS))
+    greet(lon=lax.rem(lon + PARTS - 1, PARTS))
     for k in range(1, levs):
-        greet(lev=lax.rem(lev + k, levs))
+        if k != levs // 2:
+            greet(lev=lax.rem(lev + k, levs))
 
     @pl.when(lat > 0)
     def _():
         greet(lat=lat - 1)
 
-        @pl.when(south_filtered & (lon != PARTS - 1))
-        def _():
-            greet(lat=lat - 1, lon=PARTS - 1)
+        @pl.when(south_filtered)
+        def _():
+            greet(lat=lat - 1, lon=PARTS - 1, lev=far)
 
     @pl.when(lat < lats - 1)
     def _():
         greet(lat=lat + 1)
 
-        @pl.when(north_filtered & (lon != 0))
-        def _():
-            greet(lat=lat + 1, lon=0)
+        @pl.when(north_filtered)
+        def _():
+            greet(lat=lat + 1, lon=0, lev=far)
 
     input_copies = [
         pltpu.make_async_copy(src, dst, input_sem.at[k])
@@ -209,8 +212,8 @@
 
     count = lambda condition: jnp.where(condition, 1, 0)
     below, above = lat > 0, lat < lats - 1
-    arrivals = PARTS - 1 + levs - 1 + count(below) + count(above)
-    arrivals += (PARTS - 1) * count(polar & ((below & (lon == 0)) | (above & (lon == PARTS - 1))))
+    arrivals = PARTS + 2 + levs - 2 + count(below) + count(above)
+    arrivals += PARTS * count(polar & ((below & (lon == 0)) | (above & (lon == PARTS - 1))))
     pl.semaphore_wait(barrier, arrivals)
 
     def send(src, dst, send_sem, recv_sem, **where):
@@ -218,16 +221,17 @@
             src_ref=src, dst_ref=dst, send_sem=send_sem, recv_sem=recv_sem,
             device_id=where, device_id_type=MESH)
 
+    order = (4, 5, 3, 6, 2, 7, 1, 0)
     circ_copies = [
         send(pack.at[lax.rem(lon + k, PARTS)], circles.at[lon], circ_send.at[k], circ_recv.at[k],
-             lon=lax.rem(lon + k, PARTS))
-        for k in range(1, PARTS)
-    ]
-
-    @pl.when(polar)
-    def _():
-        for k in (4, 3, 5, 2, 6, 1, 7):
-            circ_copies[k - 1].start()
+             lon=lax.rem(lon + k, PARTS), lev=far)
+        for k in order
+    ]
+
+    @pl.when(polar)
+    def _():
+        for copy in circ_copies:
+            copy.start()
 
     edge_copies = [
         send(edge_out.at[0], edge_in.at[0], edge_send.at[0], edge_recv.at[0], lon=lax.rem(lon + PARTS - 1, PARTS)),
@@ -242,7 +246,7 @@
 
     @pl.when(lat == 0)
     def _():
-        send(row_out.at[0], row_in.at[0], row_send.at[0], row_recv.at[0], lon=across).start()
+        send(row_out.at[0], pole_in.at[lon], row_send.at[0], pole_recv.at[lon], lon=0, lev=far).start()
 
     @pl.when(lat < lats - 1)
     def _():
@@ -250,7 +254,7 @@
 
     @pl.when(lat == lats - 1)
     def _():
-        send(row_out.at[1], row_in.at[1], row_send.at[1], row_recv.at[1], lon=across).start()
+        send(row_out.at[1], pole_in.at[lon], row_send.at[1], pole_recv.at[lon], lon=PARTS - 1, lev=far).start()
 
     @pl.when(polar)
     def _():
@@ -260,17 +264,16 @@
         for j in range(2):
             rank = jnp.where(own == 0, row + j, lats * rows - 1 - (row + j))
             cuts.append(cut_ref[own, rank].astype(jnp.float32))
-        circles[lon] = pack[lon]
         for copy in table_copies:
             copy.wait()
-        for k in range(1, PARTS):
-            circ_copies[k - 1].wait_recv()
+        for copy in circ_copies:
+            copy.wait_recv()
         filter_blocks(circles, filtered, stack, table, twists, cuts, width)
 
     home_copies = [
         send(filtered.at[lax.rem(lon + k, PARTS)], home.at[lon], home_send.at[k], home_recv.at[k],
-             lon=lax.rem(lon + k, PARTS))
-        for k in range(1, PARTS)
+             lon=lax.rem(lon + k, PARTS), lev=far)
+        for k in order
     ]
 
     def ghost_copy(d, side, **where):
@@ -282,59 +285,51 @@
             for d in range(PARTS):
                 @pl.when(lat > 0)
                 def _():
-                    act(ghost_copy(d, 1, lat=lat - 1, lon=d))
-
-                if d != PARTS // 2:
-                    @pl.when(lat == 0)
-                    def _():
-                        act(ghost_copy(d, 0, lon=(d + PARTS // 2) % PARTS))
+                    act(ghost_copy(d, 1, lat=lat - 1, lon=d, lev=far))
+
+                @pl.when(lat == 0)
+                def _():
+                    act(ghost_copy(d, 0, lon=(d + PARTS // 2) % PARTS, lev=far))
 
         @pl.when(polar & (lon == PARTS - 1))
         def _():
             for d in range(PARTS):
                 @pl.when(lat < lats - 1)
                 def _():
-                    act(ghost_copy(d, 0, lat=lat + 1, lon=d))
-
-                if d != PARTS // 2 - 1:
-                    @pl.when(lat == lats - 1)
-                    def _():
-                        act(ghost_copy(d, 1, lon=(d + PARTS // 2) % PARTS))
-
-    @pl.when(polar & (lon == 0))
-    def _():
-        for d in range(PARTS):
-            ghost_out[d, 0:1, :] = filtered[d, 2:3, :]
-            ghost_out[d, 1:2, :] = filtered[d, 4:5, :]
-
-    @pl.when(polar & (lon == PARTS - 1))
-    def _():
-        for d in range(PARTS):
-            ghost_out[d, 0:1, :] = filtered[d, 3:4, :]
-            ghost_out[d, 1:2, :] = filtered[d, 5:6, :]
-
-    self_south = (lat == 0) & (lon == 0)
-    self_north = (lat == lats - 1) & (lon == PARTS - 1)
-
-    @pl.when(polar)
-    def _():
-        for k in (4, 3, 5, 2, 6, 1, 7):
-            home_copies[k - 1].start()
+                    act(ghost_copy(d, 0, lat=lat + 1, lon=d, lev=far))
+
+                @pl.when(lat == lats - 1)
+                def _():
+                    act(ghost_copy(d, 1, lon=(d + PARTS // 2) % PARTS, lev=far))
+
+    for edge_owner, row, at_pole in ((0, 0, lat == 0), (PARTS - 1, 1, lat == lats - 1)):
+        @pl.when(polar & (lon == edge_owner))
+        def _():
+            for d in range(PARTS):
+                ghost_out[d, 0:1, :] = filtered[d, 2 + row : 3 + row, :]
+                ghost_out[d, 1:2, :] = filtered[d, 4 + row : 5 + row, :]
+                ghost_out[d, 2:3, :] = jnp.zeros((1, lanes), jnp.float32)
+
+            @pl.when(at_pole)
+            def _():
+                for d in range(PARTS):
+                    pltpu.make_async_copy(row_out.at[row], pole_in.at[d], pole_recv.at[d]).wait()
+                for d in range(PARTS):
+                    ghost_out[d, 2:3, :] = pole_in[d, 2:3, :]
+
+    @pl.when(polar)
+    def _():
+        for copy in home_copies:
+            copy.start()
 
     ghost_copies(lambda copy: copy.start())
-
-    @pl.when(self_south)
-    def _():
-        ghost[0] = ghost_out[PARTS // 2]
-
-    @pl.when(self_north)
-    def _():
-        ghost[1] = ghost_out[PARTS // 2 - 1]
 
     for copy in edge_copies:
         copy.wait_recv()
-    for side in range(2):
-        pltpu.make_async_copy(row_out.at[side], row_in.at[side], row_recv.at[side]).wait()
+    for side, present in ((0, lat > 0), (1, lat < lats - 1)):
+        @pl.when(present)
+        def _():
+            pltpu.make_async_copy(row_out.at[side], row_in.at[side], row_recv.at[side]).wait()
 
     def with_edges(value, f):
         east, west = edge_in[0][:, f : f + 1], edge_in[1][:, f : f + 1]
@@ -355,18 +350,17 @@
 
     @pl.when(polar)
     def _():
-        home[lon] = filtered[lon]
-        for k in range(1, PARTS):
-            home_copies[k - 1].wait_recv()
+        for copy in home_copies:
+            copy.wait_recv()
         for e in range(PARTS):
             for f in range(3):
                 smooth[f, 2 * e : 2 * e + 2, :] = home[e, 2 * f : 2 * f + 2, :]
 
-    @pl.when(south_filtered & jnp.logical_not(self_south))
+    @pl.when(south_filtered)
     def _():
         pltpu.make_async_copy(ghost_out.at[0], ghost.at[0], ghost_recv.at[0]).wait()
 
-    @pl.when(north_filtered & jnp.logical_not(self_north))
+    @pl.when(north_filtered)
     def _():
         pltpu.make_async_copy(ghost_out.at[0], ghost.at[1], ghost_recv.at[1]).wait()
 
@@ -382,7 +376,7 @@
         pole = (lat == 0) if side == 0 else (lat == lats - 1)
         gv = jnp.where(wanted, ghost[side, 0:1, :], row_in[side, 0:1, :])
         gt = jnp.where(wanted, ghost[side, 1:2, :], row_in[side, 1:2, :])
-        gp = row_in[side, 2:3, :]
+        gp = jnp.where(pole, ghost[side, 2:3, :], row_in[side, 2:3, :])
         ext[0, at : at + 1, :] = jnp.where(pole, -gv, gv)
         ext[1, at : at + 1, :] = -heat_link_multiplier * gt - gp * (1.0 / levs)
     merid_v = ext[0, 9 : 9 + rows, :] - ext[0, 7 : 7 + rows, :]
@@ -468,12 +462,13 @@
                 pltpu.VMEM((2, rows, 128), f32),
                 pltpu.VMEM((2, 3, lanes), f32),
                 pltpu.VMEM((2, 3, lanes), f32),
-                pltpu.VMEM((PARTS, 2, lanes), f32),
-                pltpu.VMEM((2, 2, lanes), f32),
+                pltpu.VMEM((PARTS, 3, lanes), f32),
+                pltpu.VMEM((PARTS, 3, lanes), f32),
+                pltpu.VMEM((2, 3, lanes), f32),
                 pltpu.VMEM((2, rows + 16, lanes), f32),
                 pltpu.VMEM((rows, lanes), f32),
                 pltpu.VMEM((levs, rows, lanes), f32),
-                dma((5,)), dma((2,)), dma((2,)), dma((2,)), dma((2,)), dma((2,)),
+                dma((5,)), dma((2,)), dma((2,)), dma((2,)), dma((2,)), dma((2,)), dma((PARTS,)),
                 dma((PARTS,)), dma((PARTS,)), dma((PARTS,)), dma((PARTS,)),
                 dma((PARTS,)), dma((2,)), dma((levs,)), dma((levs,)),
             ],

time: 49.6 us -> 47.2 us (0.952)
  the two profiles are of different devices: /device:TPU:24 before, /device:TPU:62 now
where the time goes in v3:
time: 47.2 us; the launch traced here: 47 us
  Pallas kernels  46.3 us (98%)
  between operations  0.64 us (1%)
    pallas_call x1, Pallas kernels, local(): pl.pallas_call(functools.partial(kernel, sizes), name='adjoint_step', out...  44.8 us
    pallas_call x1, Pallas kernels, local(): pl.pallas_call(unpack, name='hand_on', out_shape=[jax.ShapeDtypeStruct(ad...  1.56 us

profile of v3, /device:TPU:62, one launch (start us, length us, event | category | flops | bytes accessed | tf_op | source)
XLA Modules:
  0.0 47.0 jit_solution(827033606653305676)
XLA Ops:
  0.6 44.8 %adjoint_step.1.packed = f32[4,16,512]{2,1,0:T(8,128)} custom-call(f32[1,16,450]{2,1,0:T(8,128)} %u_hbm.1, f32[1,16,450]{2,1,0:T(8,128)} %v_hbm.1, f32[1,16,450]{2,1,0:T(8,128)} %t_hbm.1, f32[16,450]{1,0:T(8,128)} %p_hbm.1, f32[1,16,450]{2,1,0:T(8,128)} %g_hbm.1, s32[2,64]{1,0:T(2,128)} %cut_ref.1, bf16[2,512,1024]{2,1,0:T(8,128)(2,1)} %constant.4.clone.table_hbm, ...), custom_call_target="tpu_custom_call" | custom-call | tf_op jit(solution)/shard_map/adjoint_step/pallas_call | solution.py:440
  45.4 1.6 %hand_on.1 = (f32[1,16,450]{2,1,0:T(8,128)}, f32[1,16,450]{2,1,0:T(8,128)}, f32[1,16,450]{2,1,0:T(8,128)}, f32[16,450]{1,0:T(8,128)}) custom-call(f32[4,16,512]{2,1,0:T(8,128)} %adjoint_step.1.packed), custom_call_target="tpu_custom_call" | custom-call | tf_op jit(solution)/shard_map/hand_on/pallas_call | solution.py:478

commit v4 on v3

--- a/solution.py
+++ b/solution.py
@@ -39,7 +39,7 @@
     both = np.concatenate([np.where(live, np.cos(angle), 0.0), np.where(live, np.sin(angle), 0.0)], axis=1)
     high = both.astype(np.float32).astype(ml_dtypes.bfloat16)
     low = (both - high.astype(np.float64)).astype(np.float32).astype(ml_dtypes.bfloat16)
-    residue = np.arange(8)
+    residue = np.arange(16) // 2
     twist = 2.0 * np.pi * ((residue[:, None] * position[None, :]) % (width * PARTS)) / (width * PARTS)
     twists = np.stack([np.cos(twist), np.sin(twist)]).astype(np.float32)
     return np.stack([high, low]), twists
@@ -58,8 +58,21 @@
     return lead[:rows] + lead[rows:] + rest
 
 
-def filter_blocks(blocks, result, stack, table, twists, cuts, width):
-    rows, lanes = blocks.shape[1:]
+def damping(cuts, lanes, width):
+    q = lax.broadcasted_iota(jnp.int32, (16, lanes), 1)
+    row = lax.broadcasted_iota(jnp.int32, (16, lanes), 0)
+    residue = lax.shift_right_logical(row, 1)
+    cut = jnp.where(row == 2 * residue, cuts[0], cuts[1])
+    wave = PARTS * q + residue
+    wave = jnp.minimum(wave, PARTS * width - wave).astype(jnp.float32)
+    ratio = cut / jnp.maximum(wave, 1.0)
+    weight = jnp.where((residue == 0) | (residue == 4), 1.0, 2.0) * (1.0 / (PARTS * width))
+    factor = jnp.where(wave <= cut, 1.0, ratio * ratio) * weight
+    return jnp.where(q < width, factor, 0.0)
+
+
+def filter_blocks(blocks, result, stack, table, twists, factor):
+    lanes = blocks.shape[-1]
     x = [blocks[d] for d in range(PARTS)]
     a = [x[d] + x[d + 4] for d in range(4)]
     b = [x[d] - x[d + 4] for d in range(4)]
@@ -74,61 +87,37 @@
         (even - odd, None),
     ]
     for r, (re, im) in enumerate(waves):
-        if r == 0:
-            new_re, new_im = re, jnp.zeros_like(re)
-        else:
-            c, s = twists[0, r : r + 1, :], twists[1, r : r + 1, :]
-            new_re = re * c if im is None else re * c + im * s
-            new_im = -re * s if im is None else im * c - re * s
-        stack[8 * r : 8 * r + rows, :] = new_re
-        stack[40 + 8 * r : 40 + 8 * r + rows, :] = new_im
+        stack[2 * r : 2 * r + 2, :] = re
+        stack[16 + 2 * r : 18 + 2 * r, :] = jnp.zeros_like(re) if im is None else im
+    c, s = twists[0], twists[1]
+    re, im = stack[:16], stack[16:]
+    stack[:16] = re * c + im * s
+    stack[16:] = im * c - re * s
     first = wave_product(stack, table)
-    q = lax.broadcasted_iota(jnp.int32, (8, lanes), 1)
-    row = lax.broadcasted_iota(jnp.int32, (8, lanes), 0)
-    cut = jnp.where(lax.rem(row, 2) == 0, cuts[0], cuts[1])
-    for r in range(5):
-        wave = PARTS * q + r
-        wave = jnp.minimum(wave, PARTS * width - wave).astype(jnp.float32)
-        ratio = cut / jnp.maximum(wave, 1.0)
-        weight = (1.0 if r in (0, 4) else 2.0) / (PARTS * width)
-        factor = jnp.where(wave <= cut, 1.0, ratio * ratio) * weight
-        factor = jnp.where(q < width, factor, 0.0)
-        lo, hi = 8 * r, 40 + 8 * r
-        re = first[lo : lo + 8, :lanes] + first[hi : hi + 8, lanes:]
-        im = first[hi : hi + 8, :lanes] - first[lo : lo + 8, lanes:]
-        stack[lo : lo + 8, :] = re * factor
-        stack[hi : hi + 8, :] = im * factor
+    stack[:16] = (first[:16, :lanes] + first[16:, lanes:]) * factor
+    stack[16:] = (first[16:, :lanes] - first[:16, lanes:]) * factor
     second = wave_product(stack, table)
-    back = []
-    for r in range(5):
-        lo, hi = 8 * r, 40 + 8 * r
-        re = second[lo : lo + 8, :lanes] - second[hi : hi + 8, lanes:]
-        if r == 0:
-            back.append((re, None))
-            continue
-        im = second[hi : hi + 8, :lanes] + second[lo : lo + 8, lanes:]
-        c, s = twists[0, r : r + 1, :], twists[1, r : r + 1, :]
-        back.append((re * c - im * s, None if r == 4 else im * c + re * s))
-    r0, r4 = back[0][0], back[4][0]
-    (r1, i1), (r2, i2), (r3, i3) = back[1], back[2], back[3]
+    re = second[:16, :lanes] - second[16:, lanes:]
+    im = second[16:, :lanes] + second[:16, lanes:]
+    back_re, back_im = re * c - im * s, im * c + re * s
+    r0, r1, r2, r3, r4 = (back_re[2 * r : 2 * r + 2] for r in range(5))
+    i1, i2, i3 = (back_im[2 * r : 2 * r + 2] for r in range(1, 4))
     plus, minus = r0 + r4, r0 - r4
-    even_a, even_b = plus + r2, plus - r2
-    odd_a, odd_b = minus - i2, minus + i2
+    base = [plus + r2, minus - i2, plus - r2, minus + i2]
     half = [
         r1 + r3,
         ((r1 - r3) - (i1 + i3)) * ROOT_HALF,
         i3 - i1,
         ((r3 - r1) - (i1 + i3)) * ROOT_HALF,
     ]
-    base = [even_a, odd_a, even_b, odd_b]
     for d in range(4):
-        result[d] = (base[d] + half[d])[:rows]
-        result[d + 4] = (base[d] - half[d])[:rows]
+        result[d] = base[d] + half[d]
+        result[d + 4] = base[d] - half[d]
 
 
 def kernel(sizes, u_hbm, v_hbm, t_hbm, p_hbm, g_hbm, cut_ref, table_hbm, twists_hbm, packed,
            u_ref, v_ref, t_ref, p_ref, g_ref, twists, table, raw, pack, circles, stack, filtered, home, smooth,
-           edge_out, edge_in, row_out, row_in, pole_in, ghost_out, ghost, ext, height, heights,
+           edge_out, edge_in, row_out, row_in, pole_in, ghost_v_out, ghost_t_out, ghost_v, ghost_t, ext, height, heights,
            input_sem, table_sem, edge_send, edge_recv, row_send, row_recv, pole_recv, circ_send, circ_recv,
            home_send, home_recv, ghost_send, ghost_recv, lev_send, lev_recv):
     lats, lons, levs, polar_ranks = sizes
@@ -206,9 +195,15 @@
 
     @pl.when(polar)
     def _():
-        for e in range(PARTS):
-            for f, value in enumerate((raw_u, raw_v, raw_t)):
-                pack[e, 2 * f : 2 * f + 2, :] = value[2 * e : 2 * e + 2]
+        stack[...] = jnp.zeros_like(stack)
+        for f, value in enumerate((raw_u, raw_v, raw_t)):
+            for e in range(PARTS):
+                pack[f, e] = value[2 * e : 2 * e + 2]
+
+    latitude = (lat * rows + lax.broadcasted_iota(jnp.int32, (rows, 128), 0)).astype(jnp.float32)
+    latitude = ((latitude + 0.5) / (lats * rows) - 0.5) * jnp.float32(math.pi)
+    scale = (zonal_courant / jnp.cos(latitude))[:, :1]
+    coriolis = (coriolis_scale * jnp.sin(latitude))[:, :1]
 
     count = lambda condition: jnp.where(condition, 1, 0)
     below, above = lat > 0, lat < lats - 1
@@ -223,15 +218,17 @@
 
     order = (4, 5, 3, 6, 2, 7, 1, 0)
     circ_copies = [
-        send(pack.at[lax.rem(lon + k, PARTS)], circles.at[lon], circ_send.at[k], circ_recv.at[k],
-             lon=lax.rem(lon + k, PARTS), lev=far)
-        for k in order
+        [send(pack.at[f, lax.rem(lon + k, PARTS)], circles.at[f, lon], circ_send.at[f, k], circ_recv.at[f, k],
+              lon=lax.rem(lon + k, PARTS), lev=far)
+         for k in order]
+        for f in range(3)
     ]
 
     @pl.when(polar)
     def _():
-        for copy in circ_copies:
-            copy.start()
+        for copies in circ_copies:
+            for copy in copies:
+                copy.start()
 
     edge_copies = [
         send(edge_out.at[0], edge_in.at[0], edge_send.at[0], edge_recv.at[0], lon=lax.rem(lon + PARTS - 1, PARTS)),
@@ -256,73 +253,85 @@
     def _():
         send(row_out.at[1], pole_in.at[lon], row_send.at[1], pole_recv.at[lon], lon=PARTS - 1, lev=far).start()
 
-    @pl.when(polar)
-    def _():
-        own = jnp.where(lat < polar_ranks, 0, 1)
-        row = lat * rows + 2 * lon
-        cuts = []
-        for j in range(2):
-            rank = jnp.where(own == 0, row + j, lats * rows - 1 - (row + j))
-            cuts.append(cut_ref[own, rank].astype(jnp.float32))
-        for copy in table_copies:
-            copy.wait()
-        for copy in circ_copies:
-            copy.wait_recv()
-        filter_blocks(circles, filtered, stack, table, twists, cuts, width)
-
     home_copies = [
-        send(filtered.at[lax.rem(lon + k, PARTS)], home.at[lon], home_send.at[k], home_recv.at[k],
-             lon=lax.rem(lon + k, PARTS), lev=far)
-        for k in order
-    ]
-
-    def ghost_copy(d, side, **where):
-        return send(ghost_out.at[d], ghost.at[side], ghost_send.at[d], ghost_recv.at[side], **where)
-
-    def ghost_copies(act):
+        [send(filtered.at[f, lax.rem(lon + k, PARTS)], home.at[f, lon], home_send.at[f, k], home_recv.at[f, k],
+              lon=lax.rem(lon + k, PARTS), lev=far)
+         for k in order]
+        for f in range(3)
+    ]
+
+    def ghost_copies(g, act):
+        out, into = ((ghost_v_out, ghost_v), (ghost_t_out, ghost_t))[g]
+
+        def copy(d, side, **where):
+            return send(out.at[d], into.at[side], ghost_send.at[g, d], ghost_recv.at[g, side], **where)
+
         @pl.when(polar & (lon == 0))
         def _():
             for d in range(PARTS):
                 @pl.when(lat > 0)
                 def _():
-                    act(ghost_copy(d, 1, lat=lat - 1, lon=d, lev=far))
+                    act(copy(d, 1, lat=lat - 1, lon=d, lev=far))
 
                 @pl.when(lat == 0)
                 def _():
-                    act(ghost_copy(d, 0, lon=(d + PARTS // 2) % PARTS, lev=far))
+                    act(copy(d, 0, lon=(d + PARTS // 2) % PARTS, lev=far))
 
         @pl.when(polar & (lon == PARTS - 1))
         def _():
             for d in range(PARTS):
                 @pl.when(lat < lats - 1)
                 def _():
-                    act(ghost_copy(d, 0, lat=lat + 1, lon=d, lev=far))
+                    act(copy(d, 0, lat=lat + 1, lon=d, lev=far))
 
                 @pl.when(lat == lats - 1)
                 def _():
-                    act(ghost_copy(d, 1, lon=(d + PARTS // 2) % PARTS, lev=far))
-
-    for edge_owner, row, at_pole in ((0, 0, lat == 0), (PARTS - 1, 1, lat == lats - 1)):
-        @pl.when(polar & (lon == edge_owner))
-        def _():
-            for d in range(PARTS):
-                ghost_out[d, 0:1, :] = filtered[d, 2 + row : 3 + row, :]
-                ghost_out[d, 1:2, :] = filtered[d, 4 + row : 5 + row, :]
-                ghost_out[d, 2:3, :] = jnp.zeros((1, lanes), jnp.float32)
-
-            @pl.when(at_pole)
-            def _():
-                for d in range(PARTS):
-                    pltpu.make_async_copy(row_out.at[row], pole_in.at[d], pole_recv.at[d]).wait()
-                for d in range(PARTS):
-                    ghost_out[d, 2:3, :] = pole_in[d, 2:3, :]
+                    act(copy(d, 1, lon=(d + PARTS // 2) % PARTS, lev=far))
+
+    def start(copy):
+        copy.start()
 
     @pl.when(polar)
     def _():
-        for copy in home_copies:
-            copy.start()
-
-    ghost_copies(lambda copy: copy.start())
+        own = jnp.where(lat < polar_ranks, 0, 1)
+        first_row = lat * rows + 2 * lon
+        cuts = []
+        for j in range(2):
+            rank = jnp.where(own == 0, first_row + j, lats * rows - 1 - (first_row + j))
+            cuts.append(cut_ref[own, rank].astype(jnp.float32))
+        factor = damping(cuts, lanes, width)
+        for copy in table_copies:
+            copy.wait()
+        for f in range(3):
+            for copy in circ_copies[f]:
+                copy.wait_recv()
+            filter_blocks(circles.at[f], filtered.at[f], stack, table, twists, factor)
+            if f == 0:
+                for copy in home_copies[f]:
+                    copy.start()
+                continue
+            for edge_owner, row, at_pole in ((0, 0, lat == 0), (PARTS - 1, 1, lat == lats - 1)):
+                @pl.when(lon == edge_owner)
+                def _():
+                    for d in range(PARTS):
+                        if f == 1:
+                            ghost_v_out[d] = filtered[f, d, row : row + 1, :]
+                        else:
+                            ghost_t_out[d, 0:1, :] = filtered[f, d, row : row + 1, :]
+                    if f == 1:
+                        for d in range(PARTS):
+                            ghost_t_out[d, 1:2, :] = jnp.zeros((1, lanes), jnp.float32)
+
+                        @pl.when(at_pole)
+                        def _():
+                            for d in range(PARTS):
+                                pltpu.make_async_copy(row_out.at[row], pole_in.at[d], pole_recv.at[d]).wait()
+                            for d in range(PARTS):
+                                ghost_t_out[d, 1:2, :] = pole_in[d, 2:3, :]
+
+            ghost_copies(f - 1, start)
+            for copy in home_copies[f]:
+                copy.start()
 
     for copy in edge_copies:
         copy.wait_recv()
@@ -343,45 +352,41 @@
         smooth[1] = raw_v
         smooth[2] = with_edges(raw_t, 1)
 
-    latitude = (lat * rows + lax.broadcasted_iota(jnp.int32, (rows, 128), 0)).astype(jnp.float32)
-    latitude = ((latitude + 0.5) / (lats * rows) - 0.5) * jnp.float32(math.pi)
-    scale = (zonal_courant / jnp.cos(latitude))[:, :1]
-    coriolis = (coriolis_scale * jnp.sin(latitude))[:, :1]
-
-    @pl.when(polar)
-    def _():
-        for copy in home_copies:
-            copy.wait_recv()
-        for e in range(PARTS):
-            for f in range(3):
-                smooth[f, 2 * e : 2 * e + 2, :] = home[e, 2 * f : 2 * f + 2, :]
-
-    @pl.when(south_filtered)
-    def _():
-        pltpu.make_async_copy(ghost_out.at[0], ghost.at[0], ghost_recv.at[0]).wait()
-
-    @pl.when(north_filtered)
-    def _():
-        pltpu.make_async_copy(ghost_out.at[0], ghost.at[1], ghost_recv.at[1]).wait()
+    def gather(f):
+        @pl.when(polar)
+        def _():
+            for copy in home_copies[f]:
+                copy.wait_recv()
+            for e in range(PARTS):
+                smooth[f, 2 * e : 2 * e + 2, :] = home[f, e]
+
+    poles = (lat == 0, lat == lats - 1)
+
+    def ghosts(g):
+        out, into = ((ghost_v_out, ghost_v), (ghost_t_out, ghost_t))[g]
+        picked = []
+        for side, wanted in ((0, south_filtered), (1, north_filtered)):
+            @pl.when(wanted)
+            def _():
+                pltpu.make_async_copy(out.at[0], into.at[side], ghost_recv.at[g, side]).wait()
+
+            picked.append(jnp.where(wanted, into[side, 0:1, :], row_in[side, g : g + 1, :]))
+        return picked
+
+    def merid(f, main, south, north):
+        ext[f, 8 : 8 + rows, :] = main
+        ext[f, 7:8, :] = south
+        ext[f, 8 + rows : 9 + rows, :] = north
+        return ext[f, 9 : 9 + rows, :] - ext[f, 7 : 7 + rows, :]
 
     def zonal(value):
         return pltpu.roll(value, lanes - 1, 1) - pltpu.roll(value, 1, 1)
 
-    fu, fv, ft = smooth[0], smooth[1], smooth[2]
-    div = -heat_link_multiplier * ft - pres * (1.0 / levs)
-    ext[0, 8 : 8 + rows, :] = fv
-    ext[1, 8 : 8 + rows, :] = div
-    for side, at in ((0, 7), (1, 8 + rows)):
-        wanted = south_filtered if side == 0 else north_filtered
-        pole = (lat == 0) if side == 0 else (lat == lats - 1)
-        gv = jnp.where(wanted, ghost[side, 0:1, :], row_in[side, 0:1, :])
-        gt = jnp.where(wanted, ghost[side, 1:2, :], row_in[side, 1:2, :])
-        gp = jnp.where(pole, ghost[side, 2:3, :], row_in[side, 2:3, :])
-        ext[0, at : at + 1, :] = jnp.where(pole, -gv, gv)
-        ext[1, at : at + 1, :] = -heat_link_multiplier * gt - gp * (1.0 / levs)
-    merid_v = ext[0, 9 : 9 + rows, :] - ext[0, 7 : 7 + rows, :]
-    merid_div = ext[1, 9 : 9 + rows, :] - ext[1, 7 : 7 + rows, :]
-    bar = scale * zonal(fu) + merid_courant * merid_v
+    gather(0)
+    gather(1)
+    fu, fv = smooth[0], smooth[1]
+    beyond = [jnp.where(poles[side], -g, g) for side, g in enumerate(ghosts(0))]
+    bar = scale * zonal(fu) + merid_courant * merid(0, fv, *beyond)
     height[...] = bar
     lev_copies = [
         send(height, heights.at[k], lev_send.at[k], lev_recv.at[k], lev=lax.rem(lev + k, levs))
@@ -389,9 +394,16 @@
     ]
     for copy in lev_copies:
         copy.start()
-    packed[0] = (raw_u - coriolis * fv - scale * zonal(div))
-    packed[1] = (raw_v + coriolis * fu - merid_courant * merid_div)
-    packed[2] = (raw_t + bar + scale * zonal(flow * ft))
+    gather(2)
+    ft = smooth[2]
+    div = -heat_link_multiplier * ft - pres * (1.0 / levs)
+    beyond = []
+    for side, g in enumerate(ghosts(1)):
+        gp = jnp.where(poles[side], ghost_t[side, 1:2, :], row_in[side, 2:3, :])
+        beyond.append(-heat_link_multiplier * g - gp * (1.0 / levs))
+    packed[0] = raw_u - coriolis * fv - scale * zonal(div)
+    packed[1] = raw_v + coriolis * fu - merid_courant * merid(1, div, *beyond)
+    packed[2] = raw_t + bar + scale * zonal(flow * ft)
 
     for copy in edge_copies:
         copy.wait_send()
@@ -400,12 +412,12 @@
 
     @pl.when(polar)
     def _():
-        for copy in circ_copies:
-            copy.wait_send()
-        for copy in home_copies:
-            copy.wait_send()
-
-    ghost_copies(lambda copy: copy.wait_send())
+        for copies in circ_copies + home_copies:
+            for copy in copies:
+                copy.wait_send()
+
+    for g in range(2):
+        ghost_copies(g, lambda copy: copy.wait_send())
     total = raw_p + bar
     for copy in lev_copies:
         copy.wait_recv()
@@ -436,7 +448,7 @@
         vmem = pl.BlockSpec(memory_space=pltpu.VMEM)
         anywhere = pl.BlockSpec(memory_space=pl.ANY)
         f32, dma = jnp.float32, pltpu.SemaphoreType.DMA
-        block = (PARTS, 6, lanes)
+        block = (3, PARTS, 2, lanes)
         packed = pl.pallas_call(
             functools.partial(kernel, sizes),
             name="adjoint_step",
@@ -454,7 +466,7 @@
                 pltpu.VMEM((5, rows, lanes), f32),
                 pltpu.VMEM(block, f32),
                 pltpu.VMEM(block, f32),
-                pltpu.VMEM((80, lanes), f32),
+                pltpu.VMEM((32, lanes), f32),
                 pltpu.VMEM(block, f32),
                 pltpu.VMEM(block, f32),
                 pltpu.VMEM((3, rows, lanes), f32),
@@ -463,14 +475,16 @@
                 pltpu.VMEM((2, 3, lanes), f32),
                 pltpu.VMEM((2, 3, lanes), f32),
                 pltpu.VMEM((PARTS, 3, lanes), f32),
-                pltpu.VMEM((PARTS, 3, lanes), f32),
-                pltpu.VMEM((2, 3, lanes), f32),
+                pltpu.VMEM((PARTS, 1, lanes), f32),
+                pltpu.VMEM((PARTS, 2, lanes), f32),
+                pltpu.VMEM((2, 1, lanes), f32),
+                pltpu.VMEM((2, 2, lanes), f32),
                 pltpu.VMEM((2, rows + 16, lanes), f32),
                 pltpu.VMEM((rows, lanes), f32),
                 pltpu.VMEM((levs, rows, lanes), f32),
                 dma((5,)), dma((2,)), dma((2,)), dma((2,)), dma((2,)), dma((2,)), dma((PARTS,)),
-                dma((PARTS,)), dma((PARTS,)), dma((PARTS,)), dma((PARTS,)),
-                dma((PARTS,)), dma((2,)), dma((levs,)), dma((levs,)),
+                dma((3, PARTS)), dma((3, PARTS)), dma((3, PARTS)), dma((3, PARTS)),
+                dma((2, PARTS)), dma((2, 2)), dma((levs,)), dma((levs,)),
             ],
             compiler_params=pltpu.CompilerParams(collective_id=0, has_side_effects=True),
         )(adjoint_u, adjoint_v, adjoint_temp, adjoint_pres, carrying_eastward_flow, cutoff,

time: 47.2 us -> 44.4 us (0.941)
  the two profiles are of different devices: /device:TPU:62 before, /device:TPU:1 now
where the time goes in v4:
time: 44.4 us; the launch traced here: 44.2 us
  Pallas kernels  43.5 us (98%)
  between operations  0.64 us (1%)
    pallas_call x1, Pallas kernels, local(): pl.pallas_call(functools.partial(kernel, sizes), name='adjoint_step', out...  42 us
    pallas_call x1, Pallas kernels, local(): pl.pallas_call(unpack, name='hand_on', out_shape=[jax.ShapeDtypeStruct(ad...  1.56 us

profile of v4, /device:TPU:1, one launch (start us, length us, event | category | flops | bytes accessed | tf_op | source)
XLA Modules:
  0.0 44.2 jit_solution(9734890171412455798)
XLA Ops:
  0.6 42.0 %adjoint_step.1.packed = f32[4,16,512]{2,1,0:T(8,128)} custom-call(f32[1,16,450]{2,1,0:T(8,128)} %u_hbm.1, f32[1,16,450]{2,1,0:T(8,128)} %v_hbm.1, f32[1,16,450]{2,1,0:T(8,128)} %t_hbm.1, f32[16,450]{1,0:T(8,128)} %p_hbm.1, f32[1,16,450]{2,1,0:T(8,128)} %g_hbm.1, s32[2,64]{1,0:T(2,128)} %cut_ref.1, bf16[2,512,1024]{2,1,0:T(8,128)(2,1)} %constant.4.clone.table_hbm, ...), custom_call_target="tpu_custom_call" | custom-call | tf_op jit(solution)/shard_map/adjoint_step/pallas_call | solution.py:452
  42.6 1.6 %hand_on.1 = (f32[1,16,450]{2,1,0:T(8,128)}, f32[1,16,450]{2,1,0:T(8,128)}, f32[1,16,450]{2,1,0:T(8,128)}, f32[16,450]{1,0:T(8,128)}) custom-call(f32[4,16,512]{2,1,0:T(8,128)} %adjoint_step.1.packed), custom_call_target="tpu_custom_call" | custom-call | tf_op jit(solution)/shard_map/hand_on/pallas_call | solution.py:492

commit v5 on v4

--- a/solution.py
+++ b/solution.py
@@ -115,8 +115,8 @@
         result[d + 4] = base[d] - half[d]
 
 
-def kernel(sizes, u_hbm, v_hbm, t_hbm, p_hbm, g_hbm, cut_ref, table_hbm, twists_hbm, packed,
-           u_ref, v_ref, t_ref, p_ref, g_ref, twists, table, raw, pack, circles, stack, filtered, home, smooth,
+def kernel(sizes, u_hbm, v_hbm, t_hbm, p_hbm, g_hbm, cut_hbm, table_hbm, twists_hbm, packed,
+           u_ref, v_ref, t_ref, p_ref, g_ref, cut_ref, twists, table, raw, pack, circles, stack, filtered, home, smooth,
            edge_out, edge_in, row_out, row_in, pole_in, ghost_v_out, ghost_t_out, ghost_v, ghost_t, ext, height, heights,
            input_sem, table_sem, edge_send, edge_recv, row_send, row_recv, pole_recv, circ_send, circ_recv,
            home_send, home_recv, ghost_send, ghost_recv, lev_send, lev_recv):
@@ -167,6 +167,7 @@
     table_copies = [
         pltpu.make_async_copy(twists_hbm, twists, table_sem.at[0]),
         pltpu.make_async_copy(table_hbm, table, table_sem.at[1]),
+        pltpu.make_async_copy(cut_hbm, cut_ref, table_sem.at[2]),
     ]
     for copy in input_copies:
         copy.start()
@@ -217,6 +218,7 @@
             device_id=where, device_id_type=MESH)
 
     order = (4, 5, 3, 6, 2, 7, 1, 0)
+    sequence = (1, 0, 2)
     circ_copies = [
         [send(pack.at[f, lax.rem(lon + k, PARTS)], circles.at[f, lon], circ_send.at[f, k], circ_recv.at[f, k],
               lon=lax.rem(lon + k, PARTS), lev=far)
@@ -226,8 +228,8 @@
 
     @pl.when(polar)
     def _():
-        for copies in circ_copies:
-            for copy in copies:
+        for f in sequence:
+            for copy in circ_copies[f]:
                 copy.start()
 
     edge_copies = [
@@ -293,6 +295,8 @@
 
     @pl.when(polar)
     def _():
+        for copy in table_copies:
+            copy.wait()
         own = jnp.where(lat < polar_ranks, 0, 1)
         first_row = lat * rows + 2 * lon
         cuts = []
@@ -300,9 +304,7 @@
             rank = jnp.where(own == 0, first_row + j, lats * rows - 1 - (first_row + j))
             cuts.append(cut_ref[own, rank].astype(jnp.float32))
         factor = damping(cuts, lanes, width)
-        for copy in table_copies:
-            copy.wait()
-        for f in range(3):
+        for f in sequence:
             for copy in circ_copies[f]:
                 copy.wait_recv()
             filter_blocks(circles.at[f], filtered.at[f], stack, table, twists, factor)
@@ -382,8 +384,8 @@
     def zonal(value):
         return pltpu.roll(value, lanes - 1, 1) - pltpu.roll(value, 1, 1)
 
+    gather(1)
     gather(0)
-    gather(1)
     fu, fv = smooth[0], smooth[1]
     beyond = [jnp.where(poles[side], -g, g) for side, g in enumerate(ghosts(0))]
     bar = scale * zonal(fu) + merid_courant * merid(0, fv, *beyond)
@@ -452,8 +454,8 @@
         packed = pl.pallas_call(
             functools.partial(kernel, sizes),
             name="adjoint_step",
-            out_shape=jax.ShapeDtypeStruct((4, rows, lanes), f32),
-            in_specs=[anywhere] * 5 + [pl.BlockSpec(memory_space=pltpu.SMEM)] + [anywhere] * 2,
+            out_shape=pltpu.VMEM((4, rows, lanes), f32),
+            in_specs=[anywhere] * 8,
             out_specs=vmem,
             scratch_shapes=[
                 pltpu.VMEM((1, rows, width), f32),
@@ -461,6 +463,7 @@
                 pltpu.VMEM((1, rows, width), f32),
                 pltpu.VMEM((rows, width), f32),
                 pltpu.VMEM((1, rows, width), f32),
+                pltpu.SMEM(cutoff.shape, jnp.int32),
                 pltpu.VMEM(twists.shape, f32),
                 pltpu.VMEM(table.shape, jnp.bfloat16),
                 pltpu.VMEM((5, rows, lanes), f32),
@@ -482,7 +485,7 @@
                 pltpu.VMEM((2, rows + 16, lanes), f32),
                 pltpu.VMEM((rows, lanes), f32),
                 pltpu.VMEM((levs, rows, lanes), f32),
-                dma((5,)), dma((2,)), dma((2,)), dma((2,)), dma((2,)), dma((2,)), dma((PARTS,)),
+                dma((5,)), dma((3,)), dma((2,)), dma((2,)), dma((2,)), dma((2,)), dma((PARTS,)),
                 dma((3, PARTS)), dma((3, PARTS)), dma((3, PARTS)), dma((3, PARTS)),
                 dma((2, PARTS)), dma((2, 2)), dma((levs,)), dma((levs,)),
             ],
@@ -496,7 +499,7 @@
             + [jax.ShapeDtypeStruct(adjoint_pres.shape, f32)],
             in_specs=[vmem],
             out_specs=[vmem] * 4,
-        )(packed)
+        )(pltpu.with_memory_space_constraint(packed, pltpu.VMEM))
 
     return jax.shard_map(
         local, mesh=mesh, in_specs=(field, field, field, plane, field, P()),

time: 44.4 us -> 42.1 us (0.948)
  the two profiles are of different devices: /device:TPU:1 before, /device:TPU:62 now
where the time goes in v5:
time: 42.1 us; the launch traced here: 41.9 us
  Pallas kernels  41.2 us (98%)
  between operations  0.64 us (2%)
    pallas_call x1, Pallas kernels, local(): pl.pallas_call(functools.partial(kernel, sizes), name='adjoint_step', out...  40.6 us

profile of v5, /device:TPU:62, one launch (start us, length us, event | category | flops | bytes accessed | tf_op | source)
XLA Modules:
  0.0 41.9 jit_solution(1844000435547091271)
XLA Ops:
  0.6 40.6 %adjoint_step.1.packed = f32[4,16,512]{2,1,0:T(8,128)S(1)} custom-call(f32[1,16,450]{2,1,0:T(8,128)} %u_hbm.1, f32[1,16,450]{2,1,0:T(8,128)} %v_hbm.1, f32[1,16,450]{2,1,0:T(8,128)} %t_hbm.1, f32[16,450]{1,0:T(8,128)} %p_hbm.1, f32[1,16,450]{2,1,0:T(8,128)} %g_hbm.1, s32[2,64]{1,0:T(2,128)} %cut_hbm.1, bf16[2,512,1024]{2,1,0:T(8,128)(2,1)} %constant.4.clone.table_hbm, ...), custom_call_target="tpu_custom_call" | custom-call | tf_op jit(solution)/shard_map/adjoint_step/pallas_call | solution.py:454
  41.2 0.7 %hand_on.1 = (f32[1,16,450]{2,1,0:T(8,128)}, f32[1,16,450]{2,1,0:T(8,128)}, f32[1,16,450]{2,1,0:T(8,128)}, f32[16,450]{1,0:T(8,128)}) custom-call(f32[4,16,512]{2,1,0:T(8,128)S(1)} %adjoint_step.1.packed), custom_call_target="tpu_custom_call" | custom-call | tf_op jit(solution)/shard_map/hand_on/pallas_call | solution.py:495
